TPU v7x, 32 devices: a whole 2x2x4 slice. The times are simulated.
32 devices in a mesh: gx: 8 (over z, x), gy: 4 (over y, core).
Axes of the slice: x: 2, y: 2, z: 4, core: 2. Of those that a mesh axis runs over, the one named last changes fastest.
Arguments:
- velocity_x: float32 [1024, 4, 384], P('gx', 'gy'), may hold values from -6 to 6
- velocity_z: float32 [1024, 4, 384], P('gx', 'gy'), may hold values from -6 to 6
- stress_xx: float32 [1024, 4, 384], P('gx', 'gy'), may hold values from -6 to 6
- stress_zz: float32 [1024, 4, 384], P('gx', 'gy'), may hold values from -6 to 6
- stress_xz: float32 [1024, 4, 384], P('gx', 'gy'), may hold values from -6 to 6
- material: int32 [1024, 4, 384], P('gx', 'gy'), may hold values from 0 to 15, as said below
- land_mask: int32 [1024, 4], P('gx', 'gy'), may hold values 0 or 1
- density: float32 [16], replicated, may hold values from 1 to 3
- lame_lambda: float32 [16], replicated, may hold values from 0.5 to 4
- shear_modulus: float32 [16], replicated, may hold values from 0.3 to 2
- continuation_land: float32 [26, 27], replicated, may hold values from -1.25 to 1.25
- continuation_sea: float32 [26, 27], replicated, may hold values from -1.25 to 1.25
- continuation_bottom: float32 [26, 27], replicated, may hold values from -1.25 to 1.25
Outputs:
- next_velocity_x: float32 [1024, 4, 384], P('gx', 'gy')
- next_velocity_z: float32 [1024, 4, 384], P('gx', 'gy')
- next_stress_xx: float32 [1024, 4, 384], P('gx', 'gy')
- next_stress_zz: float32 [1024, 4, 384], P('gx', 'gy')
- next_stress_xz: float32 [1024, 4, 384], P('gx', 'gy')
Inputs may be any that keep to these rules, and one draw needn't show every extreme that they name: `material`: in every vertical line the layer number never falls with depth, and it is 0 at depth index 0.
All inputs are finite; a program needn't handle non-finite values. No bound on the sum of `land_mask` on one device may be relied on, other than what follows from the above.
Results may differ from a plain program's by a relative error of at most 0.000073.
Values sent between devices are 32-bit elements; how exact they have to be, the bound alone decides.
No kernel may reach another device: no remote copies, remote signals or barrier semaphores. Data moves between devices by JAX's collectives and lax.ppermute only.
A program may use at most 64 MiB of HBM per device.

v0:
```python
import functools

import jax
import jax.numpy as jnp
import numpy as np
from jax import lax
from jax.experimental import pallas as pl
from jax.experimental.pallas import tpu as pltpu
from jax.sharding import PartitionSpec as P

time_step = 0.2
LANES = 128
VMEM = pl.BlockSpec(memory_space=pltpu.VMEM)
SMEM = pl.BlockSpec(memory_space=pltpu.SMEM)


def circulant_row(length):
    m = np.arange(length)
    m = np.where(m < length - length // 2, m, m - length)
    angle = np.pi * m / length
    tangent = np.where(m == 0, 1.0, np.tan(angle))
    return np.where(m == 0, 0.0, (1.0 - 2.0 * (m % 2)) * (np.pi / length) / tangent)


def halves(matrix):
    matrix = matrix.astype(np.float32)
    high = matrix.astype(jnp.bfloat16)
    low = (matrix - high.astype(np.float32)).astype(jnp.bfloat16)
    return jnp.asarray(np.stack([high, low]))


def lateral_constants(length):
    c = circulant_row(length)

    def block(first, second, sign, scale):
        n = len(first)
        d = np.arange(n)[None, :] - np.arange(n)[:, None]
        value = first + sign * second
        entry = value[d % n]
        return scale * (entry if sign > 0 else np.where(d < 0, -entry, entry))

    h = length // 2
    skew_half = block(c[:h], c[h:], -1, 0.5)
    u = c[:h] + c[h:]
    q = h // 2
    return (
        halves(block(u[:q], u[q:], 1, 0.25)),
        halves(block(u[:q], u[q:], -1, 0.25)),
        halves(skew_half),
    )


def depth_constants(depth, extra):
    c = circulant_row(depth + extra)
    j, k = np.arange(depth), np.arange(depth + extra)
    matrix = c[(j[:, None] - k[None, :]) % (depth + extra)]
    pad = -(-extra // 32) * 32
    boundary = np.zeros((pad, depth))
    boundary[:extra] = matrix[:, depth:].T
    return halves(matrix[:, :depth].T), halves(boundary)


def split(x):
    high = x.astype(jnp.bfloat16)
    return high, (x - high.astype(jnp.float32)).astype(jnp.bfloat16)


def times(x, right):
    high, low = split(x)

    def mm(a, b):
        return jnp.dot(a, b, preferred_element_type=jnp.float32)

    return mm(high, right[0]) + (mm(low, right[0]) + mm(high, right[1]))


def times_t(x, left):
    high, low = split(x)
    left_high, left_low = split(left)

    def mm(a, b):
        return lax.dot_general(a, b, (((1,), (1,)), ((), ())), preferred_element_type=jnp.float32)

    return mm(high, left_high) + (mm(low, left_high) + mm(high, left_low))


def fold(x):
    h = x.shape[1] // 2
    return x[:, :h] + x[:, h:], x[:, :h] - x[:, h:]


def unfold(a, b):
    return jnp.concatenate([a + b, a - b], axis=1)


def lateral(x, even_ref, odd_ref, skew_ref):
    u, w = fold(x)
    uu, uw = fold(u)
    return unfold(unfold(times(uu, even_ref), times(uw, odd_ref)), times(w, skew_ref))


def lines_of(ref, lines):
    chunks = ref.shape[0] // lines
    return [ref[pl.ds(c, lines, stride=chunks), :] for c in range(chunks)]


def put_lines(ref, chunks):
    for c, value in enumerate(chunks):
        ref[pl.ds(c, value.shape[0], stride=len(chunks)), :] = value


def turned(chunks):
    return jnp.concatenate([v.T for v in chunks], axis=0)


def send_rows(ref, first, field):
    w = field.shape[0] // ref.shape[0]
    for d in range(ref.shape[0]):
        ref[d, first : first + w, :] = field[d * w : (d + 1) * w]


def look_up(material, table_ref):
    value = jnp.full(material.shape, table_ref[0], jnp.float32)
    for layer in range(1, table_ref.shape[0]):
        value = jnp.where(material >= layer, table_ref[layer], value)
    return value


def depth_pair(first, second, land, gram_ref, inner_ref, outer_ref):
    lines = first[0].shape[0]
    both = jnp.concatenate(
        [jnp.concatenate(first, axis=1), jnp.concatenate(second, axis=1)], axis=0
    )
    pad = outer_ref.shape[1]
    top = times_t(both[:, :LANES], gram_ref[: 2 * pad])
    bottom = times_t(both[:, both.shape[1] - LANES :], gram_ref[2 * pad :])
    picked = jnp.concatenate([land, land], axis=0)[:, :pad]
    extension = jnp.where(picked, top[:, :pad], top[:, pad:]) + bottom
    out = times(both, inner_ref) + times(extension, outer_ref)

    def chunked(x):
        return [x[:, c * LANES : (c + 1) * LANES] for c in range(len(first))]

    return chunked(out[:lines]), chunked(out[lines:])


def land_of(land_ref):
    lines = land_ref.shape[1]
    return jnp.broadcast_to(land_ref[...], (LANES, lines)).T > 0


def send_kernel(xx_ref, xz_ref, out_ref):
    lines = out_ref.shape[2]
    w = out_ref.shape[1] // 2
    send_rows(out_ref, 0, turned(lines_of(xx_ref, lines)))
    send_rows(out_ref, w, turned(lines_of(xz_ref, lines)))


def middle_kernel(
    step_ref, xz_ref, zz_ref, vx_ref, vz_ref, material_ref, land_ref, gram_ref, inner_ref, outer_ref, out_ref
):
    lines = land_ref.shape[1]
    groups = out_ref.shape[0]
    layers = step_ref.shape[0]
    material = lines_of(material_ref, lines)
    depth_xz, depth_zz = depth_pair(
        lines_of(xz_ref, lines), lines_of(zz_ref, lines), land_of(land_ref), gram_ref, inner_ref, outer_ref
    )
    step = [look_up(m, step_ref) for m in material]
    w = material_ref.shape[0] * LANES // lines // groups
    for first, v_ref, d in ((0, vx_ref, depth_xz), (w, vz_ref, depth_zz)):
        mixed = [v + s * x for v, s, x in zip(lines_of(v_ref, lines), step, d)]
        send_rows(out_ref, first, turned(mixed))
    down = turned(material)
    counts = [
        jnp.sum((down < layer).astype(jnp.float32), axis=0, keepdims=True) for layer in range(1, layers)
    ]
    rows = out_ref.shape[1] - 2 * w
    counts = jnp.concatenate(counts + [counts[-1]] * (rows - layers + 1), axis=0)
    for d in range(groups):
        out_ref[d, 2 * w :, :] = counts


def lateral_kernel(in_ref, even_ref, odd_ref, skew_ref, out_ref):
    x = jnp.concatenate([in_ref[q] for q in range(in_ref.shape[0])], axis=1)
    y = lateral(x, even_ref, odd_ref, skew_ref)
    n = in_ref.shape[2]
    for q in range(out_ref.shape[0]):
        out_ref[q] = y[:, q * n : (q + 1) * n]


def velocity_kernel(place_ref, step_ref, lateral_ref, mixed_ref, out_ref):
    groups, rows, n = lateral_ref.shape
    w = rows // 2
    depth = (lax.broadcasted_iota(jnp.int32, (w, n), 0) + place_ref[0] * w).astype(jnp.float32)
    for q in range(groups):
        step = jnp.full((w, n), step_ref[0], jnp.float32)
        for layer in range(1, step_ref.shape[0]):
            interface = mixed_ref[q, rows + layer - 1 : rows + layer, :]
            step = jnp.where(depth >= interface, step_ref[layer], step)
        for first in (0, w):
            out_ref[q, first : first + w, :] = (
                mixed_ref[q, first : first + w, :] + step * lateral_ref[q, first : first + w, :]
            )


def gather_rows(ref, first, w):
    field = jnp.concatenate([ref[d, first : first + w, :] for d in range(ref.shape[0])], axis=0)
    return [field[c * LANES : (c + 1) * LANES].T for c in range(field.shape[0] // LANES)]


def depth_kernel(
    v_ref, land_ref, gram_ref, inner_ref, outer_ref, vx_ref, vz_ref, dx_ref, dz_ref
):
    w = v_ref.shape[1] // 2
    vx, vz = gather_rows(v_ref, 0, w), gather_rows(v_ref, w, w)
    put_lines(vx_ref, vx)
    put_lines(vz_ref, vz)
    dx, dz = depth_pair(vx, vz, land_of(land_ref), gram_ref, inner_ref, outer_ref)
    put_lines(dx_ref, dx)
    put_lines(dz_ref, dz)


def stress_kernel(
    lame_ref, shear_ref, in_ref, dx_ref, dz_ref, material_ref, land_ref, xx_ref, zz_ref, xz_ref,
    new_xx_ref, new_zz_ref, new_xz_ref,
):
    lines = land_ref.shape[1]
    w = in_ref.shape[1] // 2
    lateral_x, lateral_z = gather_rows(in_ref, 0, w), gather_rows(in_ref, w, w)
    land = land_of(land_ref)
    chunks = len(lateral_x)
    results = ([], [], [])
    dx, dz = lines_of(dx_ref, lines), lines_of(dz_ref, lines)
    xx, zz, xz = lines_of(xx_ref, lines), lines_of(zz_ref, lines), lines_of(xz_ref, lines)
    material = lines_of(material_ref, lines)
    for c in range(chunks):
        lame = look_up(material[c], lame_ref)
        shear = look_up(material[c], shear_ref)
        normal = lame + 2.0 * shear
        new_xx = xx[c] + time_step * (normal * lateral_x[c] + lame * dz[c])
        new_zz = zz[c] + time_step * (lame * lateral_x[c] + normal * dz[c])
        new_xz = xz[c] + time_step * shear * (dx[c] + lateral_z[c])
        if c == 0:
            surface = lax.broadcasted_iota(jnp.int32, new_zz.shape, 1) == 0
            new_zz = jnp.where(surface & land, 0.0, new_zz)
            new_xz = jnp.where(surface, 0.0, new_xz)
        for kept, value in zip(results, (new_xx, new_zz, new_xz)):
            kept.append(value)
    for ref, value in zip((new_xx_ref, new_zz_ref, new_xz_ref), results):
        put_lines(ref, value)


def call(kernel, outs, specs, args, flops, name):
    moved = sum(a.size * a.dtype.itemsize for a in (*args, *outs))
    single = len(outs) == 1
    return pl.pallas_call(
        kernel,
        out_shape=outs[0] if single else tuple(outs),
        in_specs=list(specs),
        out_specs=VMEM if single else (VMEM,) * len(outs),
        cost_estimate=pl.CostEstimate(flops=flops, bytes_accessed=moved, transcendentals=0),
        compiler_params=pltpu.CompilerParams(vmem_limit_bytes=40 << 20),
        name=name,
    )(*args)


def exchange(x):
    return lax.all_to_all(x, "gx", split_axis=0, concat_axis=0, tiled=True)


def body(
    groups,
    velocity_x,
    velocity_z,
    stress_xx,
    stress_zz,
    stress_xz,
    material,
    land_mask,
    density,
    lame_lambda,
    shear_modulus,
    continuation_land,
    continuation_sea,
    continuation_bottom,
):
    lines, _, depth = velocity_x.shape
    width = lines * groups
    extra, window = continuation_land.shape
    layers = density.shape[0]
    w = depth // groups
    f32 = jnp.float32

    def shape(*dims):
        return jax.ShapeDtypeStruct(dims, f32)

    def flat(x):
        return x.reshape(lines * depth // LANES, LANES)

    vx, vz, xx, zz, xz, material = map(
        flat, (velocity_x, velocity_z, stress_xx, stress_zz, stress_xz, material)
    )
    land = land_mask.reshape(1, lines)
    inner, outer = depth_constants(depth, extra)
    fold_matrices = lateral_constants(width)
    pad = outer.shape[1]

    def padded(g, start):
        return jnp.pad(g, ((0, pad - extra), (start, LANES - window - start)))

    gram = jnp.concatenate(
        [padded(continuation_land, 0), padded(continuation_sea, 0), padded(continuation_bottom, LANES - window)],
        axis=0,
    )
    step = time_step * (1.0 / density)
    place = lax.axis_index("gx").astype(jnp.int32).reshape(1)
    rows = -(-(layers - 1) // 8) * 8
    depth_flops = 2 * 2 * lines * depth * depth * 3
    lateral_flops = 2 * 2 * w * width * width

    packed = call(
        send_kernel, [shape(groups, 2 * w, lines)], [VMEM] * 2, (xx, xz), 1 << 20, "send"
    )
    arrived = exchange(packed)
    mixed = call(
        middle_kernel,
        [shape(groups, 2 * w + rows, lines)],
        [SMEM] + [VMEM] * 9,
        (step, xz, zz, vx, vz, material, land, gram, inner, outer),
        depth_flops,
        "middle",
    )
    mixed = exchange(mixed)
    slopes = call(
        lateral_kernel,
        [shape(groups, 2 * w, lines)],
        [VMEM] * 4,
        (arrived, *fold_matrices),
        lateral_flops,
        "lateral_stress",
    )
    moving = call(
        velocity_kernel,
        [shape(groups, 2 * w, lines)],
        [SMEM, SMEM, VMEM, VMEM],
        (place, step, slopes, mixed),
        1 << 20,
        "velocity",
    )
    settled = exchange(moving)
    slopes = call(
        lateral_kernel,
        [shape(groups, 2 * w, lines)],
        [VMEM] * 4,
        (moving, *fold_matrices),
        lateral_flops,
        "lateral_velocity",
    )
    slopes = exchange(slopes)
    like = jax.ShapeDtypeStruct(vx.shape, f32)
    next_vx, next_vz, depth_vx, depth_vz = call(
        depth_kernel,
        [like] * 4,
        [VMEM] * 5,
        (settled, land, gram, inner, outer),
        depth_flops,
        "depth",
    )
    next_xx, next_zz, next_xz = call(
        stress_kernel,
        [like] * 3,
        [SMEM, SMEM] + [VMEM] * 8,
        (lame_lambda, shear_modulus, slopes, depth_vx, depth_vz, material, land, xx, zz, xz),
        1 << 20,
        "stress",
    )
    return tuple(
        x.reshape(velocity_x.shape) for x in (next_vx, next_vz, next_xx, next_zz, next_xz)
    )


def solution(mesh):
    field = P("gx", "gy", None)
    return jax.shard_map(
        functools.partial(body, mesh.shape["gx"]),
        mesh=mesh,
        in_specs=(field,) * 6 + (P("gx", "gy"),) + (P(),) * 6,
        out_specs=(field,) * 5,
        check_vma=False,
    )
```

profile of v0, /device:TPU:0, one launch (start us, length us, event | category | flops | bytes accessed | tf_op | source)
XLA Modules:
  0.0 73.8 jit_solution(2088642280540383550)
XLA Ops:
  0.6 0.0 copy-start.2
  0.6 0.9 %copy-done.2 = f32[128,1,384]{2,1,0:T(1,128)S(1)} copy-done((f32[128,1,384]{2,1,0:T(1,128)S(1)}, f32[128,1,384]{2,1,0:T(1,128)}, u32[]{:S(2)}) %copy-start.2) | copy-done | bytes 196632
  1.6 0.9 %copy-done.7 = f32[128,1,384]{2,1,0:T(1,128)S(1)} copy-done((f32[128,1,384]{2,1,0:T(1,128)S(1)}, f32[128,1,384]{2,1,0:T(1,128)}, u32[]{:S(2)}) %copy-start.7) | copy-done | bytes 196632
  2.5 0.0 copy-start.10
  2.5 0.0 copy-start.14
  2.5 0.9 %send.1 = f32[8,96,128]{2,1,0:T(8,128)} custom-call(f32[384,128]{1,0:T(8,128)S(1)} %bitcast.16, f32[384,128]{1,0:T(8,128)S(1)} %bitcast.13), custom_call_target="tpu_custom_call" | custom-call | flops 1048576 | bytes 786432 | tf_op jit(solution)/shard_map/send/pallas_call | solution.py:257
  3.5 7.4 %all-to-all-start = ((f32[8,96,128]{2,1,0:T(8,128)}), f32[8,96,128]{2,1,0:T(8,128)S(1)}, u32[]{:S(2)}, u32[]{:S(2)}) async-start(f32[8,96,128]{2,1,0:T(8,128)} %send.1), calls=%async_computation | async-start | bytes 786432 | tf_op jit(solution)/shard_map/all_to_all | solution.py:269
  10.9 0.0 copy-done.21
  10.9 0.0 copy-start.16
  10.9 0.1 select_maximum_fusion.gram_ref
  11.1 0.6 copy-done.16
  11.7 2.6 %middle.1 = f32[8,112,128]{2,1,0:T(8,128)} custom-call(f32[16]{0:T(128)S(1)} %divide_multiply_fusion.step_ref, f32[384,128]{1,0:T(8,128)S(1)} %bitcast.14, f32[384,128]{1,0:T(8,128)S(1)} %bitcast.18, f32[384,128]{1,0:T(8,128)S(1)} %bitcast.22, f32[384,128]{1,0:T(8,128)S(1)} %bitcast.23, s32[384,128]{1,0:T(8,128)S(1)} %bitcast.20, s32[1,128]{1,0:T(1,128)S(1)} %bitcast.24, ...), custom_call_target="tpu_custom_call" | custom-call | flops 226492416 | bytes 2130496 | tf_op jit(solution)/shard_map/middle/pallas_call | solution.py:257
  14.3 0.6 copy-done.12
  14.9 7.7 %all-to-all-done.in_ref = f32[8,96,128]{2,1,0:T(8,128)S(1)} async-done(((f32[8,96,128]{2,1,0:T(8,128)}), f32[8,96,128]{2,1,0:T(8,128)S(1)}, u32[]{:S(2)}, u32[]{:S(2)}) %all-to-all-start) | async-done | bytes 393248 | tf_op jit(solution)/shard_map/all_to_all | solution.py:269
  22.6 3.6 %all-to-all-start.1 = ((f32[8,112,128]{2,1,0:T(8,128)}), f32[8,112,128]{2,1,0:T(8,128)S(1)}, u32[]{:S(2)}, u32[]{:S(2)}) async-start(f32[8,112,128]{2,1,0:T(8,128)} %middle.1), calls=%async_computation.1 | async-start | bytes 917504 | tf_op jit(solution)/shard_map/all_to_all | solution.py:269
  26.2 0.0 copy-start.5
  26.2 0.9 %copy-done.5 = bf16[2,256,256]{2,1,0:T(8,128)(2,1)S(1)} copy-done((bf16[2,256,256]{2,1,0:T(8,128)(2,1)S(1)}, bf16[2,256,256]{2,1,0:T(8,128)(2,1)}, u32[]{:S(2)}) %copy-start.5) | copy-done | bytes 262168
  27.2 0.5 lateral_stress.1.lateral_ref
  27.7 11.5 %all-to-all-done.1.mixed_ref = f32[8,112,128]{2,1,0:T(8,128)S(1)} async-done(((f32[8,112,128]{2,1,0:T(8,128)}), f32[8,112,128]{2,1,0:T(8,128)S(1)}, u32[]{:S(2)}, u32[]{:S(2)}) %all-to-all-start.1) | async-done | bytes 458784 | tf_op jit(solution)/shard_map/all_to_all | solution.py:269
  39.2 1.5 %velocity.1.in_ref = f32[8,96,128]{2,1,0:T(8,128)} custom-call(s32[1]{0:T(128)} %bitcast.place_ref, f32[16]{0:T(128)S(1)} %divide_multiply_fusion.step_ref, f32[8,96,128]{2,1,0:T(8,128)S(1)} %lateral_stress.1.lateral_ref, f32[8,112,128]{2,1,0:T(8,128)S(1)} %all-to-all-done.1.mixed_ref), custom_call_target="tpu_custom_call" | custom-call | flops 1048576 | bytes 1245252 | tf_op jit(solution)/shard_map/velocity/pallas_call | solution.py:257
  40.7 3.8 %all-to-all-start.2 = ((f32[8,96,128]{2,1,0:T(8,128)}), f32[8,96,128]{2,1,0:T(8,128)S(1)}, u32[]{:S(2)}, u32[]{:S(2)}) async-start(f32[8,96,128]{2,1,0:T(8,128)} %velocity.1.in_ref), calls=%async_computation.2 | async-start | bytes 786432 | tf_op jit(solution)/shard_map/all_to_all | solution.py:269
  44.5 2.3 %lateral_velocity.1 = f32[8,96,128]{2,1,0:T(8,128)} custom-call(f32[8,96,128]{2,1,0:T(8,128)} %velocity.1.in_ref, bf16[2,256,256]{2,1,0:T(8,128)(2,1)S(1)} %copy-done.6, bf16[2,256,256]{2,1,0:T(8,128)(2,1)S(1)} %copy-done.4, bf16[2,512,512]{2,1,0:T(8,128)(2,1)S(1)} %copy-done), custom_call_target="tpu_custom_call" | custom-call | flops 201326592 | bytes 2359296 | tf_op jit(solution)/shard_map/lateral_velocity/pallas_call | solution.py:257
  46.8 9.4 %all-to-all-done.2.v_ref = f32[8,96,128]{2,1,0:T(8,128)S(1)} async-done(((f32[8,96,128]{2,1,0:T(8,128)}), f32[8,96,128]{2,1,0:T(8,128)S(1)}, u32[]{:S(2)}, u32[]{:S(2)}) %all-to-all-start.2) | async-done | bytes 393248 | tf_op jit(solution)/shard_map/all_to_all | solution.py:269
  56.2 3.6 %all-to-all-start.3 = ((f32[8,96,128]{2,1,0:T(8,128)}), f32[8,96,128]{2,1,0:T(8,128)S(1)}, u32[]{:S(2)}, u32[]{:S(2)}) async-start(f32[8,96,128]{2,1,0:T(8,128)} %lateral_velocity.1), calls=%async_computation.3 | async-start | bytes 786432 | tf_op jit(solution)/shard_map/all_to_all | solution.py:269
  59.8 0.0 copy-done.17
  59.8 0.0 copy-start.8
  59.8 0.0 copy-start.11
  59.8 1.3 %depth.1 = (f32[384,128]{1,0:T(8,128)}, f32[384,128]{1,0:T(8,128)}, f32[384,128]{1,0:T(8,128)S(1)}, f32[384,128]{1,0:T(8,128)S(1)}) custom-call(f32[8,96,128]{2,1,0:T(8,128)S(1)} %all-to-all-done.2.v_ref, s32[1,128]{1,0:T(1,128)S(1)} %bitcast.25, f32[96,128]{1,0:T(8,128)S(1)} %copy-done.13, bf16[2,384,384]{2,1,0:T(8,128)(2,1)S(1)} %copy-done.1, ...), custom_call_target="tpu_custom_call" | custom-call | flops 226492416 | bytes 1868288 | tf_op jit(solution)/shard_map/depth/pallas_call | solution.py:257
  61.2 10.3 %all-to-all-done.3.in_ref = f32[8,96,128]{2,1,0:T(8,128)S(1)} async-done(((f32[8,96,128]{2,1,0:T(8,128)}), f32[8,96,128]{2,1,0:T(8,128)S(1)}, u32[]{:S(2)}, u32[]{:S(2)}) %all-to-all-start.3) | async-done | bytes 393248 | tf_op jit(solution)/shard_map/all_to_all | solution.py:269
  71.4 0.6 copy-done.19
  72.1 0.0 copy-done.20
  72.1 1.7 %stress.1 = (f32[384,128]{1,0:T(8,128)}, f32[384,128]{1,0:T(8,128)}, f32[384,128]{1,0:T(8,128)}) custom-call(f32[16]{0:T(128)S(1)} %copy-done.19, f32[16]{0:T(128)S(1)} %copy-done.20, f32[8,96,128]{2,1,0:T(8,128)S(1)} %all-to-all-done.3.in_ref, f32[384,128]{1,0:T(8,128)S(1)} %get-tuple-element.14.dx_ref, f32[384,128]{1,0:T(8,128)S(1)} %get-tuple-element.15.dz_ref, ...), custom_call_target="tpu_custom_call" | custom-call | flops 1048576 | bytes 2163328 | tf_op jit(solution)/shard_map/stress/pallas_call | solution.py:257
  (35 shorter events, 0.1 us)
Async XLA Ops:
  0.6 0.9 %copy-start.2 = (f32[128,1,384]{2,1,0:T(1,128)S(1)}, f32[128,1,384]{2,1,0:T(1,128)}, u32[]{:S(2)}) copy-start(f32[128,1,384]{2,1,0:T(1,128)} %param.22) | copy-start | bytes 589828
  1.6 0.9 %copy-start.7 = (f32[128,1,384]{2,1,0:T(1,128)S(1)}, f32[128,1,384]{2,1,0:T(1,128)}, u32[]{:S(2)}) copy-start(f32[128,1,384]{2,1,0:T(1,128)} %param.20) | copy-start | bytes 589828
  2.5 8.4 %copy-start.21 = (f32[26,27]{1,0:T(8,128)S(1)}, f32[26,27]{1,0:T(8,128)}, u32[]{:S(2)}) copy-start(f32[26,27]{1,0:T(8,128)} %param.30) | copy-start | bytes 8428
  2.5 8.4 %copy-start.22 = (f32[26,27]{1,0:T(8,128)S(1)}, f32[26,27]{1,0:T(8,128)}, u32[]{:S(2)}) copy-start(f32[26,27]{1,0:T(8,128)} %param.29) | copy-start | bytes 8428
  2.5 8.4 %copy-start.23 = (f32[26,27]{1,0:T(8,128)S(1)}, f32[26,27]{1,0:T(8,128)}, u32[]{:S(2)}) copy-start(f32[26,27]{1,0:T(8,128)} %param.28) | copy-start | bytes 8428
  2.5 8.5 %copy-start.9 = (f32[128,1,384]{2,1,0:T(1,128)S(1)}, f32[128,1,384]{2,1,0:T(1,128)}, u32[]{:S(2)}) copy-start(f32[128,1,384]{2,1,0:T(1,128)} %param.21) | copy-start | bytes 589828
  2.5 8.5 %copy-start.10 = (s32[128,1,384]{2,1,0:T(1,128)S(1)}, s32[128,1,384]{2,1,0:T(1,128)}, u32[]{:S(2)}) copy-start(s32[128,1,384]{2,1,0:T(1,128)} %param.23) | copy-start | bytes 589828
  2.5 8.5 %copy-start.14 = (f32[128,1,384]{2,1,0:T(1,128)S(1)}, f32[128,1,384]{2,1,0:T(1,128)}, u32[]{:S(2)}) copy-start(f32[128,1,384]{2,1,0:T(1,128)} %param.18) | copy-start | bytes 589828
  2.5 8.5 %copy-start.15 = (f32[128,1,384]{2,1,0:T(1,128)S(1)}, f32[128,1,384]{2,1,0:T(1,128)}, u32[]{:S(2)}) copy-start(f32[128,1,384]{2,1,0:T(1,128)} %param.19) | copy-start | bytes 589828
  3.5 7.5 %copy-start.24 = (f32[16]{0:T(128)S(1)}, f32[16]{0:T(128)}, u32[]{:S(2)}) copy-start(f32[16]{0:T(128)} %param.25) | copy-start | bytes 196
  3.5 7.6 %copy-start.1 = (bf16[2,384,384]{2,1,0:T(8,128)(2,1)S(1)}, bf16[2,384,384]{2,1,0:T(8,128)(2,1)}, u32[]{:S(2)}) copy-start(bf16[2,384,384]{2,1,0:T(8,128)(2,1)} %constant.23.clone.inner_ref) | copy-start | bytes 1769476
  3.5 7.6 %copy-start.3 = (f32[128,1,384]{2,1,0:T(1,128)S(1)}, f32[128,1,384]{2,1,0:T(1,128)}, u32[]{:S(2)}) copy-start(f32[128,1,384]{2,1,0:T(1,128)} %param.22) | copy-start | bytes 589828
  3.5 19.1 %all-to-all-start = ((f32[8,96,128]{2,1,0:T(8,128)}), f32[8,96,128]{2,1,0:T(8,128)S(1)}, u32[]{:S(2)}, u32[]{:S(2)}) async-start(f32[8,96,128]{2,1,0:T(8,128)} %send.1), calls=%async_computation | async-start | bytes 786432 | tf_op jit(solution)/shard_map/all_to_all | solution.py:269
  10.9 0.8 %copy-start.16 = (bf16[2,32,384]{2,1,0:T(8,128)(2,1)S(1)}, bf16[2,32,384]{2,1,0:T(8,128)(2,1)}, u32[]{:S(2)}) copy-start(bf16[2,32,384]{2,1,0:T(8,128)(2,1)} %constant.24.clone.outer_ref) | copy-start | bytes 147460
  11.0 0.7 copy-start.18
  11.7 14.5 %copy-start = (bf16[2,512,512]{2,1,0:T(8,128)(2,1)S(1)}, bf16[2,512,512]{2,1,0:T(8,128)(2,1)}, u32[]{:S(2)}) copy-start(bf16[2,512,512]{2,1,0:T(8,128)(2,1)} %constant.27.clone.skew_ref) | copy-start | bytes 3145732
  14.3 0.6 copy-start.12
  14.9 11.3 %copy-start.4 = (bf16[2,256,256]{2,1,0:T(8,128)(2,1)S(1)}, bf16[2,256,256]{2,1,0:T(8,128)(2,1)}, u32[]{:S(2)}) copy-start(bf16[2,256,256]{2,1,0:T(8,128)(2,1)} %constant.26.clone.odd_ref) | copy-start | bytes 786436
  22.6 16.6 %all-to-all-start.1 = ((f32[8,112,128]{2,1,0:T(8,128)}), f32[8,112,128]{2,1,0:T(8,128)S(1)}, u32[]{:S(2)}, u32[]{:S(2)}) async-start(f32[8,112,128]{2,1,0:T(8,128)} %middle.1), calls=%async_computation.1 | async-start | bytes 917504 | tf_op jit(solution)/shard_map/all_to_all | solution.py:269
  26.2 1.0 %copy-start.5 = (bf16[2,256,256]{2,1,0:T(8,128)(2,1)S(1)}, bf16[2,256,256]{2,1,0:T(8,128)(2,1)}, u32[]{:S(2)}) copy-start(bf16[2,256,256]{2,1,0:T(8,128)(2,1)} %constant.25.clone.even_ref) | copy-start | bytes 786436
  40.7 3.8 %copy-start.6 = (bf16[2,256,256]{2,1,0:T(8,128)(2,1)S(1)}, bf16[2,256,256]{2,1,0:T(8,128)(2,1)}, u32[]{:S(2)}) copy-start(bf16[2,256,256]{2,1,0:T(8,128)(2,1)} %constant.25.clone.even_ref) | copy-start | bytes 786436
  40.7 15.5 %all-to-all-start.2 = ((f32[8,96,128]{2,1,0:T(8,128)}), f32[8,96,128]{2,1,0:T(8,128)S(1)}, u32[]{:S(2)}, u32[]{:S(2)}) async-start(f32[8,96,128]{2,1,0:T(8,128)} %velocity.1.in_ref), calls=%async_computation.2 | async-start | bytes 786432 | tf_op jit(solution)/shard_map/all_to_all | solution.py:269
  46.8 13.0 %copy-start.13 = (f32[96,128]{1,0:T(8,128)S(1)}, f32[96,128]{1,0:T(8,128)}, u32[]{:S(2)}) copy-start(f32[96,128]{1,0:T(8,128)} %copy-done.12) | copy-start | bytes 147460
  46.8 13.0 %copy-start.17 = (bf16[2,32,384]{2,1,0:T(8,128)(2,1)S(1)}, bf16[2,32,384]{2,1,0:T(8,128)(2,1)}, u32[]{:S(2)}) copy-start(bf16[2,32,384]{2,1,0:T(8,128)(2,1)} %constant.24.clone.outer_ref) | copy-start | bytes 147460
  56.2 15.3 %all-to-all-start.3 = ((f32[8,96,128]{2,1,0:T(8,128)}), f32[8,96,128]{2,1,0:T(8,128)S(1)}, u32[]{:S(2)}, u32[]{:S(2)}) async-start(f32[8,96,128]{2,1,0:T(8,128)} %lateral_velocity.1), calls=%async_computation.3 | async-start | bytes 786432 | tf_op jit(solution)/shard_map/all_to_all | solution.py:269
  59.8 11.6 %copy-start.8 = (f32[128,1,384]{2,1,0:T(1,128)S(1)}, f32[128,1,384]{2,1,0:T(1,128)}, u32[]{:S(2)}) copy-start(f32[128,1,384]{2,1,0:T(1,128)} %param.20) | copy-start | bytes 589828
  59.8 11.6 %copy-start.11 = (s32[128,1,384]{2,1,0:T(1,128)S(1)}, s32[128,1,384]{2,1,0:T(1,128)}, u32[]{:S(2)}) copy-start(s32[128,1,384]{2,1,0:T(1,128)} %param.23) | copy-start | bytes 589828
  71.4 0.7 copy-start.19
  71.4 0.7 copy-start.20
where the time goes:
time: 74.5 us; the launch traced here: 73.8 us
  waiting for transfers between devices  38.8 us (52%)
  starting transfers between devices  18.5 us (25%)
  Pallas kernels  10.9 us (15%)
  local copies, waits for them, and re-layouts  4.79 us (6%)
  between operations  0.82 us (1%)
    all_to_all x4, waiting for transfers between devices, exchange(): return lax.all_to_all(x, 'gx', split_axis=0, concat_axis=0, tiled=True)  38.8 us
    all_to_all x4, starting transfers between devices, exchange(): return lax.all_to_all(x, 'gx', split_axis=0, concat_axis=0, tiled=True)  18.5 us
    pallas_call x7, Pallas kernels, call(): pl.pallas_call(kernel, out_shape=outs[0] if single else tuple(outs), in_s...  10.9 us
    unnamed x50, local copies, waits for them, and re-layouts  4.79 us
  transfers between devices with their start and end apart: 4, of which 4 were waited for; matrix products, arithmetic and copies ran while one was open for 0% of the time, Pallas kernels for 9%

commit v1 on v0

v1 whole, which is shorter than its diff:
```python
import functools

import jax
import jax.numpy as jnp
import numpy as np
from jax import lax
from jax.experimental import pallas as pl
from jax.experimental.pallas import tpu as pltpu
from jax.sharding import PartitionSpec as P


time_step = 0.2
LANES = 128
VMEM = pl.BlockSpec(memory_space=pltpu.VMEM)
SMEM = pl.BlockSpec(memory_space=pltpu.SMEM)
HBM = pl.BlockSpec(memory_space=pltpu.HBM)


def circulant_row(length):
    m = np.arange(length)
    m = np.where(m < length - length // 2, m, m - length)
    angle = np.pi * m / length
    tangent = np.where(m == 0, 1.0, np.tan(angle))
    return np.where(m == 0, 0.0, (1.0 - 2.0 * (m % 2)) * (np.pi / length) / tangent)


def halves(matrix):
    matrix = matrix.astype(np.float32)
    high = matrix.astype(jnp.bfloat16)
    low = (matrix - high.astype(np.float32)).astype(jnp.bfloat16)
    return jnp.asarray(np.stack([high, low]))


def lateral_constants(length):
    c = circulant_row(length)

    def block(first, second, sign, scale):
        n = len(first)
        d = np.arange(n)[None, :] - np.arange(n)[:, None]
        value = first + sign * second
        entry = value[d % n]
        return scale * (entry if sign > 0 else np.where(d < 0, -entry, entry))

    h = length // 2
    skew_half = block(c[:h], c[h:], -1, 0.5)
    u = c[:h] + c[h:]
    q = h // 2
    return (
        halves(block(u[:q], u[q:], 1, 0.25)),
        halves(block(u[:q], u[q:], -1, 0.25)),
        halves(skew_half),
    )


def depth_constants(depth, extra):
    c = circulant_row(depth + extra)
    j, k = np.arange(depth), np.arange(depth + extra)
    matrix = c[(j[:, None] - k[None, :]) % (depth + extra)]
    pad = -(-extra // 32) * 32
    boundary = np.zeros((pad, depth))
    boundary[:extra] = matrix[:, depth:].T
    return halves(matrix[:, :depth].T), halves(boundary)


def split(x):
    high = x.astype(jnp.bfloat16)
    return high, (x - high.astype(jnp.float32)).astype(jnp.bfloat16)


def times(x, right):
    high, low = split(x)

    def mm(a, b):
        return jnp.dot(a, b, preferred_element_type=jnp.float32)

    return mm(high, right[0]) + (mm(low, right[0]) + mm(high, right[1]))


def times_t(x, left):
    high, low = split(x)
    left_high, left_low = split(left)

    def mm(a, b):
        return lax.dot_general(a, b, (((1,), (1,)), ((), ())), preferred_element_type=jnp.float32)

    return mm(high, left_high) + (mm(low, left_high) + mm(high, left_low))


def fold(x):
    h = x.shape[1] // 2
    return x[:, :h] + x[:, h:], x[:, :h] - x[:, h:]


def unfold(a, b):
    return jnp.concatenate([a + b, a - b], axis=1)


def lateral(x, even_ref, odd_ref, skew_ref):
    u, w = fold(x)
    uu, uw = fold(u)
    return unfold(unfold(times(uu, even_ref), times(uw, odd_ref)), times(w, skew_ref))


def lines_of(ref, lines):
    chunks = ref.shape[0] // lines
    return [ref[pl.ds(c, lines, stride=chunks), :] for c in range(chunks)]


def put_lines(ref, chunks):
    for c, value in enumerate(chunks):
        ref[pl.ds(c, value.shape[0], stride=len(chunks)), :] = value


def turned(chunks):
    return jnp.concatenate([v.T for v in chunks], axis=0)


def send_rows(ref, first, field):
    w = field.shape[0] // ref.shape[0]
    for d in range(ref.shape[0]):
        ref[d, first : first + w, :] = field[d * w : (d + 1) * w]


def look_up(material, table_ref):
    value = jnp.full(material.shape, table_ref[0], jnp.float32)
    for layer in range(1, table_ref.shape[0]):
        value = jnp.where(material >= layer, table_ref[layer], value)
    return value


def depth_pair(first, second, land, gram, inner_ref, outer_ref):
    lines = first[0].shape[0]
    both = jnp.concatenate(
        [jnp.concatenate(first, axis=1), jnp.concatenate(second, axis=1)], axis=0
    )
    pad = outer_ref.shape[1]
    top = times_t(both[:, :LANES], gram[: 2 * pad])
    bottom = times_t(both[:, both.shape[1] - LANES :], gram[2 * pad :])
    picked = jnp.concatenate([land, land], axis=0)[:, :pad]
    extension = jnp.where(picked, top[:, :pad], top[:, pad:]) + bottom
    out = times(both, inner_ref) + times(extension, outer_ref)

    def chunked(x):
        return [x[:, c * LANES : (c + 1) * LANES] for c in range(len(first))]

    return chunked(out[:lines]), chunked(out[lines:])


def gram_of(top_land_ref, top_sea_ref, bottom_ref, pad):
    def padded(ref, start):
        extra, window = ref.shape
        return jnp.pad(ref[...], ((0, pad - extra), (start, LANES - window - start)))

    return jnp.concatenate(
        [padded(top_land_ref, 0), padded(top_sea_ref, 0), padded(bottom_ref, LANES - bottom_ref.shape[1])], axis=0
    )


def land_of(land_ref):
    lines = land_ref.shape[1]
    return jnp.broadcast_to(land_ref[...], (LANES, lines)).T > 0


def first_kernel(
    place_ref, xz_hbm, zz_hbm, inner_hbm, xx_hbm, material_hbm, vx_hbm, vz_hbm, land_hbm, top_land_hbm, top_sea_hbm,
    bottom_hbm, outer_hbm, density_hbm, *rest,
):
    (*out_refs, fields, material_ref, inner_ref, land_ref, top_land_ref, top_sea_ref, bottom_ref, outer_ref,
     density_ref, packed, sems) = rest
    groups = len(out_refs)
    lines = land_ref.shape[1]
    layers = density_ref.shape[0]
    moves = (
        (xz_hbm, fields.at[0]),
        (zz_hbm, fields.at[1]),
        (xx_hbm, fields.at[2]),
        (vx_hbm, fields.at[3]),
        (vz_hbm, fields.at[4]),
        (material_hbm, material_ref),
        (inner_hbm, inner_ref),
        (land_hbm, land_ref),
        (top_land_hbm, top_land_ref),
        (top_sea_hbm, top_sea_ref),
        (bottom_hbm, bottom_ref),
        (outer_hbm, outer_ref),
        (density_hbm, density_ref),
    )
    copies = [pltpu.make_async_copy(a, b, sems.at[i]) for i, (a, b) in enumerate(moves)]
    for i in (7, 8, 9, 10, 11, 12, 0, 1, 6, 2, 5, 3, 4):
        copies[i].start()
    for i in range(7, 13):
        copies[i].wait()
    gram = gram_of(top_land_ref, top_sea_ref, bottom_ref, outer_ref.shape[1])
    land = land_of(land_ref)
    w = fields.shape[1] * LANES // lines // groups
    copies[6].wait()
    copies[0].wait()
    copies[1].wait()
    xz = lines_of(fields.at[0], lines)
    depth_xz, depth_zz = depth_pair(
        xz, lines_of(fields.at[1], lines), land, gram, inner_ref, outer_ref
    )
    send_rows(packed, w, turned(xz))
    copies[2].wait()
    send_rows(packed, 0, turned(lines_of(fields.at[2], lines)))
    copies[5].wait()
    material = lines_of(material_ref, lines)
    down = turned(material)
    counts = [
        jnp.sum((down < layer).astype(jnp.float32), axis=0, keepdims=True) for layer in range(1, layers)
    ]
    rows = packed.shape[1] - 4 * w
    counts = jnp.concatenate(counts + [counts[-1]] * (rows - layers + 1), axis=0)
    for d in range(groups):
        packed[d, 4 * w :, :] = counts
    step = [time_step * (1.0 / look_up(m, density_ref)) for m in material]
    copies[3].wait()
    copies[4].wait()
    for first, i, d in ((2 * w, 3, depth_xz), (3 * w, 4, depth_zz)):
        mixed = [v + s * x for v, s, x in zip(lines_of(fields.at[i], lines), step, d)]
        send_rows(packed, first, turned(mixed))
    scatter_blocks(place_ref, packed, out_refs)


def scatter_blocks(place_ref, packed, out_refs):
    for s, ref in enumerate(out_refs):
        ref[...] = packed[place_ref[0] ^ s]


def collect_blocks(place_ref, in_refs, packed):
    for s, ref in enumerate(in_refs):
        packed[place_ref[0] ^ s] = ref[...]


def pencil_kernel(groups, place_ref, step_ref, even_ref, odd_ref, skew_ref, *rest):
    in_refs, out_refs, (arrived, leaving) = rest[:groups], rest[groups : 2 * groups], rest[2 * groups :]
    n = in_refs[0].shape[1]
    w = leaving.shape[1] // 4
    collect_blocks(place_ref, in_refs, arrived)
    x = jnp.concatenate([arrived[q, : 2 * w] for q in range(groups)], axis=1)
    slopes = lateral(x, even_ref, odd_ref, skew_ref)
    depth = (lax.broadcasted_iota(jnp.int32, (w, n), 0) + place_ref[0] * w).astype(jnp.float32)
    moving = []
    for q in range(groups):
        step = jnp.full((w, n), step_ref[0], jnp.float32)
        for layer in range(1, step_ref.shape[0]):
            interface = arrived[q, 4 * w + layer - 1 : 4 * w + layer, :]
            step = jnp.where(depth >= interface, step_ref[layer], step)
        step = jnp.concatenate([step, step], axis=0)
        new = arrived[q, 2 * w : 4 * w] + step * slopes[:, q * n : (q + 1) * n]
        leaving[q, : 2 * w] = new
        moving.append(new)
    slopes = lateral(jnp.concatenate(moving, axis=1), even_ref, odd_ref, skew_ref)
    for q in range(groups):
        leaving[q, 2 * w :] = slopes[:, q * n : (q + 1) * n]
    scatter_blocks(place_ref, leaving, out_refs)


def gather_rows(ref, first, w):
    field = jnp.concatenate([ref[d, first : first + w, :] for d in range(ref.shape[0])], axis=0)
    return [field[c * LANES : (c + 1) * LANES].T for c in range(field.shape[0] // LANES)]


def last_kernel(
    groups, place_ref, lame_ref, shear_ref, xx_ref, zz_ref, xz_ref, material_ref, land_ref,
    top_land_ref, top_sea_ref, bottom_ref, inner_ref, outer_ref, *rest,
):
    in_refs, (new_vx, new_vz, new_xx_ref, new_zz_ref, new_xz_ref, settled) = rest[:groups], rest[groups:]
    lines = land_ref.shape[1]
    w = settled.shape[1] // 4
    collect_blocks(place_ref, in_refs, settled)
    land = land_of(land_ref)
    gram = gram_of(top_land_ref, top_sea_ref, bottom_ref, outer_ref.shape[1])
    vx, vz, lateral_x, lateral_z = (gather_rows(settled, i * w, w) for i in range(4))
    put_lines(new_vx, vx)
    put_lines(new_vz, vz)
    dx, dz = depth_pair(vx, vz, land, gram, inner_ref, outer_ref)
    results = ([], [], [])
    xx, zz, xz = lines_of(xx_ref, lines), lines_of(zz_ref, lines), lines_of(xz_ref, lines)
    material = lines_of(material_ref, lines)
    for c in range(len(vx)):
        lame = look_up(material[c], lame_ref)
        shear = look_up(material[c], shear_ref)
        normal = lame + 2.0 * shear
        new_xx = xx[c] + time_step * (normal * lateral_x[c] + lame * dz[c])
        new_zz = zz[c] + time_step * (lame * lateral_x[c] + normal * dz[c])
        new_xz = xz[c] + time_step * shear * (dx[c] + lateral_z[c])
        if c == 0:
            surface = lax.broadcasted_iota(jnp.int32, new_zz.shape, 1) == 0
            new_zz = jnp.where(surface & land, 0.0, new_zz)
            new_xz = jnp.where(surface, 0.0, new_xz)
        for kept, value in zip(results, (new_xx, new_zz, new_xz)):
            kept.append(value)
    for ref, value in zip((new_xx_ref, new_zz_ref, new_xz_ref), results):
        put_lines(ref, value)


def call(kernel, outs, specs, args, flops, scratch=(), on_chip=True):
    moved = sum(a.size * a.dtype.itemsize for a in (*args, *outs))
    return pl.pallas_call(
        kernel,
        out_shape=tuple(pltpu.VMEM(o.shape, o.dtype) if on_chip else o for o in outs),
        in_specs=list(specs),
        out_specs=(VMEM,) * len(outs),
        scratch_shapes=list(scratch),
        cost_estimate=pl.CostEstimate(flops=flops, bytes_accessed=moved, transcendentals=0),
        compiler_params=pltpu.CompilerParams(vmem_limit_bytes=40 << 20),
    )(*args)


def hop_order(groups):
    return list(range(groups // 2, groups)) + list(range(groups // 2 - 1, 0, -1))


def exchange(blocks):
    groups = len(blocks)
    order = hop_order(groups)
    moved = {}
    for s in order:
        moved[s] = lax.ppermute(blocks[s], "gx", [(i, i ^ s) for i in range(groups)])
    return [blocks[0]] + [moved[s] for s in range(1, groups)]


def body(
    groups,
    velocity_x,
    velocity_z,
    stress_xx,
    stress_zz,
    stress_xz,
    material,
    land_mask,
    density,
    lame_lambda,
    shear_modulus,
    continuation_land,
    continuation_sea,
    continuation_bottom,
):
    lines, _, depth = velocity_x.shape
    width = lines * groups
    extra = continuation_land.shape[0]
    layers = density.shape[0]
    w = depth // groups
    f32 = jnp.float32

    def shape(*dims):
        return jax.ShapeDtypeStruct(dims, f32)

    def kept(x):
        return pltpu.with_memory_space_constraint(x, pltpu.HBM)

    def flat(x):
        return x.reshape(lines * depth // LANES, LANES)

    vx, vz, xx, zz, xz, material = map(
        flat, (velocity_x, velocity_z, stress_xx, stress_zz, stress_xz, material)
    )
    land = land_mask.reshape(1, lines)
    inner, outer = depth_constants(depth, extra)
    fold_matrices = lateral_constants(width)
    grams = (continuation_land, continuation_sea, continuation_bottom)
    step = time_step * (1.0 / density)
    place = lax.axis_index("gx").astype(jnp.int32).reshape(1)
    rows = -(-(layers - 1) // 8) * 8
    depth_flops = 2 * 2 * lines * depth * depth * 3
    lateral_flops = 2 * 2 * w * width * width
    stored = vx.shape

    leaving = call(
        first_kernel,
        [shape(4 * w + rows, lines)] * groups,
        [SMEM] + [HBM] * 13,
        (place, *map(kept, (xz, zz, inner, xx, material, vx, vz, land, *grams, outer, density))),
        depth_flops,
        [
            pltpu.VMEM((5, *stored), f32),
            pltpu.VMEM(stored, jnp.int32),
            pltpu.VMEM(inner.shape, inner.dtype),
            pltpu.VMEM(land.shape, jnp.int32),
            *(pltpu.VMEM(g.shape, f32) for g in grams),
            pltpu.VMEM(outer.shape, outer.dtype),
            pltpu.SMEM(density.shape, f32),
            pltpu.VMEM((groups, 4 * w + rows, lines), f32),
            pltpu.SemaphoreType.DMA((13,)),
        ],
    )
    arrived = exchange(leaving)
    leaving = call(
        functools.partial(pencil_kernel, groups),
        [shape(4 * w, lines)] * groups,
        [SMEM] * 2 + [VMEM] * (3 + groups),
        (place, step, *fold_matrices, *arrived),
        2 * lateral_flops,
        [
            pltpu.VMEM((groups, 4 * w + rows, lines), f32),
            pltpu.VMEM((groups, 4 * w, lines), f32),
        ],
    )
    arrived = exchange(leaving)
    results = call(
        functools.partial(last_kernel, groups),
        [shape(*stored)] * 5,
        [SMEM] * 3 + [VMEM] * (10 + groups),
        (place, lame_lambda, shear_modulus, xx, zz, xz, material, land, *grams, inner, outer, *arrived),
        depth_flops,
        [pltpu.VMEM((groups, 4 * w, lines), f32)],
        False,
    )
    return tuple(x.reshape(velocity_x.shape) for x in results)


def solution(mesh):
    field = P("gx", "gy", None)
    groups = mesh.shape["gx"]
    return jax.shard_map(
        functools.partial(body, groups),
        mesh=mesh,
        in_specs=(field,) * 6 + (P("gx", "gy"),) + (P(),) * 6,
        out_specs=(field,) * 5,
        check_vma=False,
    )
```

time: 74.5 us -> 56.2 us (0.75)
  waiting for transfers between devices: 38.8 us -> 20.2 us
  starting transfers between devices: 18.5 us -> 26.4 us
  local copies, waits for them, and re-layouts: 4.79 us -> 0.09 us
  Pallas kernels: 10.9 us -> 7.64 us
    all_to_all x4 -> x0, waiting for transfers between devices: 38.8 us -> none  [exchange(): return lax.all_to_all(x, 'gx', split_axis=0, concat_axis=0, tiled=True)]
    ppermute x0 -> x14, starting transfers between devices: none -> 26.4 us  [exchange(): lax.ppermute(blocks[s], 'gx', [(i, i ^ s) for i in range(groups)])]
    ppermute x0 -> x14, waiting for transfers between devices: none -> 20.2 us  [exchange(): lax.ppermute(blocks[s], 'gx', [(i, i ^ s) for i in range(groups)])]
    all_to_all x4 -> x0, starting transfers between devices: 18.5 us -> none  [exchange(): return lax.all_to_all(x, 'gx', split_axis=0, concat_axis=0, tiled=True)]
    unnamed x50 -> x32, local copies, waits for them, and re-layouts: 4.79 us -> 0.09 us
    pallas_call x7 -> x3, Pallas kernels: 10.9 us -> 7.64 us  [call(): pl.pallas_call(kernel, out_shape=tuple((pltpu.VMEM(o.shape, o.dtype) if o...]
  transfers between devices with their start and end apart: 4 -> 14, of which waited for: 4 -> 3; matrix products, arithmetic and copies ran while one was open for 0% -> 0% of each run, Pallas kernels for 9% -> 0%
where the time goes in v1:
time: 56.2 us; the launch traced here: 55.2 us
  starting transfers between devices  26.4 us (47%)
  waiting for transfers between devices  20.2 us (36%)
  Pallas kernels  7.64 us (14%)
  between operations  0.88 us (2%)
    ppermute x14, starting transfers between devices, exchange(): lax.ppermute(blocks[s], 'gx', [(i, i ^ s) for i in range(groups)])  26.4 us
    ppermute x14, waiting for transfers between devices, exchange(): lax.ppermute(blocks[s], 'gx', [(i, i ^ s) for i in range(groups)])  20.2 us
    pallas_call x3, Pallas kernels, call(): pl.pallas_call(kernel, out_shape=tuple((pltpu.VMEM(o.shape, o.dtype) if o...  7.64 us
  transfers between devices with their start and end apart: 14, of which 3 were waited for; matrix products, arithmetic and copies ran while one was open for 0% of the time, Pallas kernels for 0%

profile of v1, /device:TPU:0, one launch (start us, length us, event | category | flops | bytes accessed | tf_op | source)
XLA Modules:
  0.0 55.2 jit_solution(7687165720591104486)
XLA Ops:
  0.6 0.0 copy-start.1
  0.6 0.0 copy-start.6
  0.7 0.0 copy-start.7
  0.7 3.2 %shard_map.209 = (f32[208,128]{1,0:T(8,128)S(1)}, f32[208,128]{1,0:T(8,128)S(1)}, f32[208,128]{1,0:T(8,128)S(1)}, f32[208,128]{1,0:T(8,128)S(1)}, f32[208,128]{1...) custom-call(s32[1]{0:T(128)} %bitcast.place_ref, f32[384,128]{1,0:T(8,128)} %bitcast.17, ...), custom_call_target="tpu_custom_call" | custom-call | flops 226492416 | bytes 2679596 | tf_op jit(solution)/shard_map/pallas_call | solution.py:300
  3.9 3.0 %collective-permute-start = (f32[208,128]{1,0:T(8,128)S(1)}, f32[208,128]{1,0:T(8,128)S(1)}, u32[]{:S(2)}, u32[]{:S(2)}) collective-permute-start(f32[208,128]{1,0:T(8,128)S(1)} %get-tuple-element.27), channel_id=1, source_target_pairs={{0,4},{4,0},{8,12},{12,8},{16,20},{20,16},{24,28},{28,24},{1,5},{5... | collective-permute-start | bytes 319496 | tf_op jit(solution)/shard_map/ppermute | solution.py:320
  7.0 1.6 %collective-permute-start.1 = (f32[208,128]{1,0:T(8,128)S(1)}, f32[208,128]{1,0:T(8,128)S(1)}, u32[]{:S(2)}, u32[]{:S(2)}) collective-permute-start(f32[208,128]{1,0:T(8,128)S(1)} %get-tuple-element.28), channel_id=1, source_target_pairs={{0,8},{4,12},{8,0},{12,4},{16,24},{20,28},{24,16},{28,20},{1,9},{5... | collective-permute-start | bytes 319496 | tf_op jit(solution)/shard_map/ppermute | solution.py:320
  8.5 3.0 %collective-permute-start.3 = (f32[208,128]{1,0:T(8,128)S(1)}, f32[208,128]{1,0:T(8,128)S(1)}, u32[]{:S(2)}, u32[]{:S(2)}) collective-permute-start(f32[208,128]{1,0:T(8,128)S(1)} %get-tuple-element.30), channel_id=1, source_target_pairs={{0,16},{4,20},{8,24},{12,28},{16,0},{20,4},{24,8},{28,12},{1,17},{... | collective-permute-start | bytes 319496 | tf_op jit(solution)/shard_map/ppermute | solution.py:320
  11.5 1.3 %collective-permute-start.4 = (f32[208,128]{1,0:T(8,128)S(1)}, f32[208,128]{1,0:T(8,128)S(1)}, u32[]{:S(2)}, u32[]{:S(2)}) collective-permute-start(f32[208,128]{1,0:T(8,128)S(1)} %get-tuple-element.31), channel_id=1, source_target_pairs={{0,20},{4,16},{8,28},{12,24},{16,4},{20,0},{24,12},{28,8},{1,21},{... | collective-permute-start | bytes 319496 | tf_op jit(solution)/shard_map/ppermute | solution.py:320
  12.8 3.6 %collective-permute-start.5 = (f32[208,128]{1,0:T(8,128)S(1)}, f32[208,128]{1,0:T(8,128)S(1)}, u32[]{:S(2)}, u32[]{:S(2)}) collective-permute-start(f32[208,128]{1,0:T(8,128)S(1)} %get-tuple-element.32), channel_id=1, source_target_pairs={{0,24},{4,28},{8,16},{12,20},{16,8},{20,12},{24,0},{28,4},{1,25},{... | collective-permute-start | bytes 319496 | tf_op jit(solution)/shard_map/ppermute | solution.py:320
  16.4 0.0 collective-permute-start.6
  16.5 0.0 collective-permute-done.3.rest_4_
  16.5 11.2 %collective-permute-done.4.rest_5_ = f32[208,128]{1,0:T(8,128)S(1)} collective-permute-done((f32[208,128]{1,0:T(8,128)S(1)}, f32[208,128]{1,0:T(8,128)S(1)}, u32[]{:S(2)}, u32[]{:S(2)}) %collective-permute-start.4) | collective-permute-done | bytes 106528 | tf_op jit(solution)/shard_map/ppermute | solution.py:320
  27.8 0.0 copy-start
  27.8 0.0 copy-start.2
  27.8 0.0 copy-start.3
  27.8 0.0 copy-start.4
  27.8 0.0 copy-start.5
  27.8 0.0 copy-start.8
  27.8 0.0 copy-start.9
  27.9 0.0 copy-start.10
  27.9 0.0 copy-start.11
  27.9 1.8 %shard_map.210 = (f32[192,128]{1,0:T(8,128)S(1)}, f32[192,128]{1,0:T(8,128)S(1)}, f32[192,128]{1,0:T(8,128)S(1)}, f32[192,128]{1,0:T(8,128)S(1)}, f32[192,128]{1...) custom-call(s32[1]{0:T(128)} %bitcast.place_ref, ...), custom_call_target="tpu_custom_call" | custom-call | flops 402653184 | bytes 3211332 | tf_op jit(solution)/shard_map/pallas_call | solution.py:300
  29.7 0.9 %collective-permute-start.7 = (f32[192,128]{1,0:T(8,128)S(1)}, f32[192,128]{1,0:T(8,128)S(1)}, u32[]{:S(2)}, u32[]{:S(2)}) collective-permute-start(f32[192,128]{1,0:T(8,128)S(1)} %get-tuple-element.35), channel_id=1, source_target_pairs={{0,4},{4,0},{8,12},{12,8},{16,20},{20,16},{24,28},{28,24},{1,5},{5... | collective-permute-start | bytes 294920 | tf_op jit(solution)/shard_map/ppermute | solution.py:320
  30.6 4.0 %collective-permute-start.8 = (f32[192,128]{1,0:T(8,128)S(1)}, f32[192,128]{1,0:T(8,128)S(1)}, u32[]{:S(2)}, u32[]{:S(2)}) collective-permute-start(f32[192,128]{1,0:T(8,128)S(1)} %get-tuple-element.36), channel_id=1, source_target_pairs={{0,8},{4,12},{8,0},{12,4},{16,24},{20,28},{24,16},{28,20},{1,9},{5... | collective-permute-start | bytes 294920 | tf_op jit(solution)/shard_map/ppermute | solution.py:320
  34.6 0.9 %collective-permute-start.9 = (f32[192,128]{1,0:T(8,128)S(1)}, f32[192,128]{1,0:T(8,128)S(1)}, u32[]{:S(2)}, u32[]{:S(2)}) collective-permute-start(f32[192,128]{1,0:T(8,128)S(1)} %get-tuple-element.37), channel_id=1, source_target_pairs={{0,12},{4,8},{8,4},{12,0},{16,28},{20,24},{24,20},{28,16},{1,13},{... | collective-permute-start | bytes 294920 | tf_op jit(solution)/shard_map/ppermute | solution.py:320
  35.5 3.3 %collective-permute-start.10 = (f32[192,128]{1,0:T(8,128)S(1)}, f32[192,128]{1,0:T(8,128)S(1)}, u32[]{:S(2)}, u32[]{:S(2)}) collective-permute-start(f32[192,128]{1,0:T(8,128)S(1)} %get-tuple-element.38), channel_id=1, source_target_pairs={{0,16},{4,20},{8,24},{12,28},{16,0},{20,4},{24,8},{28,12},{1,17},{... | collective-permute-start | bytes 294920 | tf_op jit(solution)/shard_map/ppermute | solution.py:320
  38.8 0.0 collective-permute-start.11
  38.8 2.4 %collective-permute-start.12 = (f32[192,128]{1,0:T(8,128)S(1)}, f32[192,128]{1,0:T(8,128)S(1)}, u32[]{:S(2)}, u32[]{:S(2)}) collective-permute-start(f32[192,128]{1,0:T(8,128)S(1)} %get-tuple-element.40), channel_id=1, source_target_pairs={{0,24},{4,28},{8,16},{12,20},{16,8},{20,12},{24,0},{28,4},{1,25},{... | collective-permute-start | bytes 294920 | tf_op jit(solution)/shard_map/ppermute | solution.py:320
  41.2 2.4 %collective-permute-start.13 = (f32[192,128]{1,0:T(8,128)S(1)}, f32[192,128]{1,0:T(8,128)S(1)}, u32[]{:S(2)}, u32[]{:S(2)}) collective-permute-start(f32[192,128]{1,0:T(8,128)S(1)} %get-tuple-element.41), channel_id=1, source_target_pairs={{0,28},{4,24},{8,20},{12,16},{16,12},{20,8},{24,4},{28,0},{1,29},{... | collective-permute-start | bytes 294920 | tf_op jit(solution)/shard_map/ppermute | solution.py:320
  43.6 6.5 %collective-permute-done.10.rest_4_ = f32[192,128]{1,0:T(8,128)S(1)} collective-permute-done((f32[192,128]{1,0:T(8,128)S(1)}, f32[192,128]{1,0:T(8,128)S(1)}, u32[]{:S(2)}, u32[]{:S(2)}) %collective-permute-start.10) | collective-permute-done | bytes 98336 | tf_op jit(solution)/shard_map/ppermute | solution.py:320
  50.1 2.4 %collective-permute-done.11.rest_5_ = f32[192,128]{1,0:T(8,128)S(1)} collective-permute-done((f32[192,128]{1,0:T(8,128)S(1)}, f32[192,128]{1,0:T(8,128)S(1)}, u32[]{:S(2)}, u32[]{:S(2)}) %collective-permute-start.11) | collective-permute-done | bytes 98336 | tf_op jit(solution)/shard_map/ppermute | solution.py:320
  52.6 2.6 %shard_map.211 = (f32[384,128]{1,0:T(8,128)}, f32[384,128]{1,0:T(8,128)}, f32[384,128]{1,0:T(8,128)}, f32[384,128]{1,0:T(8,128)}, f32[384,128]{1,0:T(8,128)}) custom-call(s32[1]{0:T(128)} %bitcast.place_ref, f32[16]{0:T(128)S(1)} %copy-done.13, f32[16]{0:T(128)S(1)} %copy-done.14, f32[384,128]{1,0:T(8,128)S(1)} %bitcast.14, f32[384,128]{1,0:T(8,128)S(1)} %bitcast.16, ...), custom_call_target="tpu_custom_call" | custom-call | flops 226492416 | bytes 3203948 | tf_op jit(solution)/shard_map/pallas_call | solution.py:300
  (32 shorter events, 0.1 us)
Async XLA Ops:
  0.6 27.1 %copy-start.1 = (bf16[2,512,512]{2,1,0:T(8,128)(2,1)S(1)}, bf16[2,512,512]{2,1,0:T(8,128)(2,1)}, u32[]{:S(2)}) copy-start(bf16[2,512,512]{2,1,0:T(8,128)(2,1)} %constant.24.clone.skew_ref) | copy-start | bytes 3145732
  0.6 27.1 %copy-start.6 = (bf16[2,256,256]{2,1,0:T(8,128)(2,1)S(1)}, bf16[2,256,256]{2,1,0:T(8,128)(2,1)}, u32[]{:S(2)}) copy-start(bf16[2,256,256]{2,1,0:T(8,128)(2,1)} %constant.23.clone.odd_ref) | copy-start | bytes 786436
  0.7 27.1 %copy-start.7 = (bf16[2,256,256]{2,1,0:T(8,128)(2,1)S(1)}, bf16[2,256,256]{2,1,0:T(8,128)(2,1)}, u32[]{:S(2)}) copy-start(bf16[2,256,256]{2,1,0:T(8,128)(2,1)} %constant.22.clone.even_ref) | copy-start | bytes 786436
  3.9 8.9 %collective-permute-start = (f32[208,128]{1,0:T(8,128)S(1)}, f32[208,128]{1,0:T(8,128)S(1)}, u32[]{:S(2)}, u32[]{:S(2)}) collective-permute-start(f32[208,128]{1,0:T(8,128)S(1)} %get-tuple-element.27), channel_id=1, source_target_pairs={{0,4},{4,0},{8,12},{12,8},{16,20},{20,16},{24,28},{28,24},{1,5},{5... | collective-permute-start | bytes 319496 | tf_op jit(solution)/shard_map/ppermute | solution.py:320
  7.0 9.5 %collective-permute-start.1 = (f32[208,128]{1,0:T(8,128)S(1)}, f32[208,128]{1,0:T(8,128)S(1)}, u32[]{:S(2)}, u32[]{:S(2)}) collective-permute-start(f32[208,128]{1,0:T(8,128)S(1)} %get-tuple-element.28), channel_id=1, source_target_pairs={{0,8},{4,12},{8,0},{12,4},{16,24},{20,28},{24,16},{28,20},{1,9},{5... | collective-permute-start | bytes 319496 | tf_op jit(solution)/shard_map/ppermute | solution.py:320
  8.5 7.9 %collective-permute-start.2 = (f32[208,128]{1,0:T(8,128)S(1)}, f32[208,128]{1,0:T(8,128)S(1)}, u32[]{:S(2)}, u32[]{:S(2)}) collective-permute-start(f32[208,128]{1,0:T(8,128)S(1)} %get-tuple-element.29), channel_id=1, source_target_pairs={{0,12},{4,8},{8,4},{12,0},{16,28},{20,24},{24,20},{28,16},{1,13},{... | collective-permute-start | bytes 319496 | tf_op jit(solution)/shard_map/ppermute | solution.py:320
  8.5 8.0 %collective-permute-start.3 = (f32[208,128]{1,0:T(8,128)S(1)}, f32[208,128]{1,0:T(8,128)S(1)}, u32[]{:S(2)}, u32[]{:S(2)}) collective-permute-start(f32[208,128]{1,0:T(8,128)S(1)} %get-tuple-element.30), channel_id=1, source_target_pairs={{0,16},{4,20},{8,24},{12,28},{16,0},{20,4},{24,8},{28,12},{1,17},{... | collective-permute-start | bytes 319496 | tf_op jit(solution)/shard_map/ppermute | solution.py:320
  11.5 16.2 %collective-permute-start.4 = (f32[208,128]{1,0:T(8,128)S(1)}, f32[208,128]{1,0:T(8,128)S(1)}, u32[]{:S(2)}, u32[]{:S(2)}) collective-permute-start(f32[208,128]{1,0:T(8,128)S(1)} %get-tuple-element.31), channel_id=1, source_target_pairs={{0,20},{4,16},{8,28},{12,24},{16,4},{20,0},{24,12},{28,8},{1,21},{... | collective-permute-start | bytes 319496 | tf_op jit(solution)/shard_map/ppermute | solution.py:320
  12.8 3.7 %copy-start.15 = (f32[16]{0:T(128)S(1)}, f32[16]{0:T(128)}, u32[]{:S(2)}) copy-start(f32[16]{0:T(128)} %density_hbm.1) | copy-start | bytes 196
  12.8 14.9 %collective-permute-start.5 = (f32[208,128]{1,0:T(8,128)S(1)}, f32[208,128]{1,0:T(8,128)S(1)}, u32[]{:S(2)}, u32[]{:S(2)}) collective-permute-start(f32[208,128]{1,0:T(8,128)S(1)} %get-tuple-element.32), channel_id=1, source_target_pairs={{0,24},{4,28},{8,16},{12,20},{16,8},{20,12},{24,0},{28,4},{1,25},{... | collective-permute-start | bytes 319496 | tf_op jit(solution)/shard_map/ppermute | solution.py:320
  16.4 11.3 %collective-permute-start.6 = (f32[208,128]{1,0:T(8,128)S(1)}, f32[208,128]{1,0:T(8,128)S(1)}, u32[]{:S(2)}, u32[]{:S(2)}) collective-permute-start(f32[208,128]{1,0:T(8,128)S(1)} %get-tuple-element.33), channel_id=1, source_target_pairs={{0,28},{4,24},{8,20},{12,16},{16,12},{20,8},{24,4},{28,0},{1,29},{... | collective-permute-start | bytes 319496 | tf_op jit(solution)/shard_map/ppermute | solution.py:320
  27.8 24.7 %copy-start = (bf16[2,384,384]{2,1,0:T(8,128)(2,1)S(1)}, bf16[2,384,384]{2,1,0:T(8,128)(2,1)}, u32[]{:S(2)}) copy-start(bf16[2,384,384]{2,1,0:T(8,128)(2,1)} %constant.20.clone.inner_hbm.inner_ref) | copy-start | bytes 1769476
  27.8 24.7 %copy-start.2 = (f32[128,1,384]{2,1,0:T(1,128)S(1)}, f32[128,1,384]{2,1,0:T(1,128)}, u32[]{:S(2)}) copy-start(f32[128,1,384]{2,1,0:T(1,128)} %param.20) | copy-start | bytes 589828
  27.8 24.7 %copy-start.3 = (f32[128,1,384]{2,1,0:T(1,128)S(1)}, f32[128,1,384]{2,1,0:T(1,128)}, u32[]{:S(2)}) copy-start(f32[128,1,384]{2,1,0:T(1,128)} %param.21) | copy-start | bytes 589828
  27.8 24.7 %copy-start.4 = (f32[128,1,384]{2,1,0:T(1,128)S(1)}, f32[128,1,384]{2,1,0:T(1,128)}, u32[]{:S(2)}) copy-start(f32[128,1,384]{2,1,0:T(1,128)} %param.22) | copy-start | bytes 589828
  27.8 24.7 %copy-start.5 = (s32[128,1,384]{2,1,0:T(1,128)S(1)}, s32[128,1,384]{2,1,0:T(1,128)}, u32[]{:S(2)}) copy-start(s32[128,1,384]{2,1,0:T(1,128)} %param.23) | copy-start | bytes 589828
  27.8 24.7 %copy-start.8 = (bf16[2,32,384]{2,1,0:T(8,128)(2,1)S(1)}, bf16[2,32,384]{2,1,0:T(8,128)(2,1)}, u32[]{:S(2)}) copy-start(bf16[2,32,384]{2,1,0:T(8,128)(2,1)} %constant.21.clone.outer_hbm.outer_ref) | copy-start | bytes 147460
  27.8 24.7 %copy-start.9 = (f32[26,27]{1,0:T(8,128)S(1)}, f32[26,27]{1,0:T(8,128)}, u32[]{:S(2)}) copy-start(f32[26,27]{1,0:T(8,128)} %top_land_ref.1) | copy-start | bytes 8428
  27.9 24.7 %copy-start.10 = (f32[26,27]{1,0:T(8,128)S(1)}, f32[26,27]{1,0:T(8,128)}, u32[]{:S(2)}) copy-start(f32[26,27]{1,0:T(8,128)} %top_sea_ref.1) | copy-start | bytes 8428
  27.9 24.7 %copy-start.11 = (f32[26,27]{1,0:T(8,128)S(1)}, f32[26,27]{1,0:T(8,128)}, u32[]{:S(2)}) copy-start(f32[26,27]{1,0:T(8,128)} %bottom_ref.1) | copy-start | bytes 8428
  29.7 9.1 %collective-permute-start.7 = (f32[192,128]{1,0:T(8,128)S(1)}, f32[192,128]{1,0:T(8,128)S(1)}, u32[]{:S(2)}, u32[]{:S(2)}) collective-permute-start(f32[192,128]{1,0:T(8,128)S(1)} %get-tuple-element.35), channel_id=1, source_target_pairs={{0,4},{4,0},{8,12},{12,8},{16,20},{20,16},{24,28},{28,24},{1,5},{5... | collective-permute-start | bytes 294920 | tf_op jit(solution)/shard_map/ppermute | solution.py:320
  30.6 10.5 %collective-permute-start.8 = (f32[192,128]{1,0:T(8,128)S(1)}, f32[192,128]{1,0:T(8,128)S(1)}, u32[]{:S(2)}, u32[]{:S(2)}) collective-permute-start(f32[192,128]{1,0:T(8,128)S(1)} %get-tuple-element.36), channel_id=1, source_target_pairs={{0,8},{4,12},{8,0},{12,4},{16,24},{20,28},{24,16},{28,20},{1,9},{5... | collective-permute-start | bytes 294920 | tf_op jit(solution)/shard_map/ppermute | solution.py:320
  34.6 9.0 %collective-permute-start.9 = (f32[192,128]{1,0:T(8,128)S(1)}, f32[192,128]{1,0:T(8,128)S(1)}, u32[]{:S(2)}, u32[]{:S(2)}) collective-permute-start(f32[192,128]{1,0:T(8,128)S(1)} %get-tuple-element.37), channel_id=1, source_target_pairs={{0,12},{4,8},{8,4},{12,0},{16,28},{20,24},{24,20},{28,16},{1,13},{... | collective-permute-start | bytes 294920 | tf_op jit(solution)/shard_map/ppermute | solution.py:320
  35.5 14.6 %collective-permute-start.10 = (f32[192,128]{1,0:T(8,128)S(1)}, f32[192,128]{1,0:T(8,128)S(1)}, u32[]{:S(2)}, u32[]{:S(2)}) collective-permute-start(f32[192,128]{1,0:T(8,128)S(1)} %get-tuple-element.38), channel_id=1, source_target_pairs={{0,16},{4,20},{8,24},{12,28},{16,0},{20,4},{24,8},{28,12},{1,17},{... | collective-permute-start | bytes 294920 | tf_op jit(solution)/shard_map/ppermute | solution.py:320
  38.8 13.7 %collective-permute-start.11 = (f32[192,128]{1,0:T(8,128)S(1)}, f32[192,128]{1,0:T(8,128)S(1)}, u32[]{:S(2)}, u32[]{:S(2)}) collective-permute-start(f32[192,128]{1,0:T(8,128)S(1)} %get-tuple-element.39), channel_id=1, source_target_pairs={{0,20},{4,16},{8,28},{12,24},{16,4},{20,0},{24,12},{28,8},{1,21},{... | collective-permute-start | bytes 294920 | tf_op jit(solution)/shard_map/ppermute | solution.py:320
  38.8 13.7 %collective-permute-start.12 = (f32[192,128]{1,0:T(8,128)S(1)}, f32[192,128]{1,0:T(8,128)S(1)}, u32[]{:S(2)}, u32[]{:S(2)}) collective-permute-start(f32[192,128]{1,0:T(8,128)S(1)} %get-tuple-element.40), channel_id=1, source_target_pairs={{0,24},{4,28},{8,16},{12,20},{16,8},{20,12},{24,0},{28,4},{1,25},{... | collective-permute-start | bytes 294920 | tf_op jit(solution)/shard_map/ppermute | solution.py:320
  41.2 11.4 %copy-start.12 = (s32[128,1]{0,1:T(1,128)S(1)}, s32[128,1]{0,1:T(1,128)}, u32[]{:S(2)}) copy-start(s32[128,1]{0,1:T(1,128)} %param.24) | copy-start | bytes 1540
  41.2 11.4 %copy-start.13 = (f32[16]{0:T(128)S(1)}, f32[16]{0:T(128)}, u32[]{:S(2)}) copy-start(f32[16]{0:T(128)} %lame_ref.1) | copy-start | bytes 196
  41.2 11.4 %copy-start.14 = (f32[16]{0:T(128)S(1)}, f32[16]{0:T(128)}, u32[]{:S(2)}) copy-start(f32[16]{0:T(128)} %shear_ref.1) | copy-start | bytes 196
  41.2 11.3 %collective-permute-start.13 = (f32[192,128]{1,0:T(8,128)S(1)}, f32[192,128]{1,0:T(8,128)S(1)}, u32[]{:S(2)}, u32[]{:S(2)}) collective-permute-start(f32[192,128]{1,0:T(8,128)S(1)} %get-tuple-element.41), channel_id=1, source_target_pairs={{0,28},{4,24},{8,20},{12,16},{16,12},{20,8},{24,4},{28,0},{1,29},{... | collective-permute-start | bytes 294920 | tf_op jit(solution)/shard_map/ppermute | solution.py:320

commit v2 on v1

--- a/solution.py
+++ b/solution.py
@@ -115,17 +115,47 @@
     return jnp.concatenate([v.T for v in chunks], axis=0)
 
 
-def send_rows(ref, first, field):
-    w = field.shape[0] // ref.shape[0]
-    for d in range(ref.shape[0]):
-        ref[d, first : first + w, :] = field[d * w : (d + 1) * w]
-
-
-def look_up(material, table_ref):
-    value = jnp.full(material.shape, table_ref[0], jnp.float32)
-    for layer in range(1, table_ref.shape[0]):
-        value = jnp.where(material >= layer, table_ref[layer], value)
-    return value
+def share_rows(depth, groups):
+    shared = 2 * depth // (3 * groups)
+    own = (depth - groups // 2 * shared) // groups
+    assert own * groups + shared * (groups // 2) == depth
+    return own, shared
+
+
+def send_rows(own_ref, shared_ref, slot, field):
+    groups, halves_ = own_ref.shape[0], shared_ref.shape[0]
+    own, shared = share_rows(field.shape[0], groups)
+    for d in range(groups):
+        own_ref[d, slot * own : (slot + 1) * own, :] = field[d * own : (d + 1) * own]
+    for r in range(halves_):
+        start = groups * own + r * shared
+        shared_ref[r, slot * shared : (slot + 1) * shared, :] = field[start : start + shared]
+
+
+def spread(table, shape):
+    return jnp.broadcast_to(jnp.pad(table, ((0, 0), (0, LANES - table.shape[1]))), shape)
+
+
+def look_up(material, table):
+    return jnp.take_along_axis(spread(table, material.shape), material, axis=1, mode="promise_in_bounds")
+
+
+def interfaces_of(down, layers):
+    depth = down.shape[0]
+    packed = down.astype(jnp.float32).astype(jnp.bfloat16)
+    blocks = [packed[i : i + 16] for i in range(0, depth, 16)]
+    reach = 256 // (layers - 1)
+    totals = [0.0]
+    for layer in range(1, layers):
+        total = 0.0
+        for first in range(0, len(blocks), reach):
+            part = None
+            for block in blocks[first : first + reach]:
+                value = jnp.minimum(block, jnp.bfloat16(layer))
+                part = value if part is None else part + value
+            total = total + part.astype(jnp.float32)
+        totals.append(jnp.sum(total, axis=0, keepdims=True))
+    return [depth - (b - a) for a, b in zip(totals, totals[1:])]
 
 
 def depth_pair(first, second, land, gram, inner_ref, outer_ref):
@@ -163,13 +193,13 @@
 
 def first_kernel(
     place_ref, xz_hbm, zz_hbm, inner_hbm, xx_hbm, material_hbm, vx_hbm, vz_hbm, land_hbm, top_land_hbm, top_sea_hbm,
-    bottom_hbm, outer_hbm, density_hbm, *rest,
+    bottom_hbm, outer_hbm, density_hbm, lame_hbm, shear_hbm, *rest,
 ):
     (*out_refs, fields, material_ref, inner_ref, land_ref, top_land_ref, top_sea_ref, bottom_ref, outer_ref,
-     density_ref, packed, sems) = rest
-    groups = len(out_refs)
+     density_ref, lame_ref, shear_ref, packed, shared, sems) = rest
+    groups = packed.shape[0]
     lines = land_ref.shape[1]
-    layers = density_ref.shape[0]
+    layers = density_ref.shape[1]
     moves = (
         (xz_hbm, fields.at[0]),
         (zz_hbm, fields.at[1]),
@@ -184,107 +214,157 @@
         (bottom_hbm, bottom_ref),
         (outer_hbm, outer_ref),
         (density_hbm, density_ref),
+        (lame_hbm, lame_ref),
+        (shear_hbm, shear_ref),
     )
     copies = [pltpu.make_async_copy(a, b, sems.at[i]) for i, (a, b) in enumerate(moves)]
-    for i in (7, 8, 9, 10, 11, 12, 0, 1, 6, 2, 5, 3, 4):
+    for i in (7, 8, 9, 10, 11, 12, 13, 14, 0, 1, 6, 5, 3, 4, 2):
         copies[i].start()
-    for i in range(7, 13):
+    for i in range(7, 15):
         copies[i].wait()
     gram = gram_of(top_land_ref, top_sea_ref, bottom_ref, outer_ref.shape[1])
     land = land_of(land_ref)
-    w = fields.shape[1] * LANES // lines // groups
-    copies[6].wait()
-    copies[0].wait()
-    copies[1].wait()
+    for i in (0, 1, 6, 5):
+        copies[i].wait()
     xz = lines_of(fields.at[0], lines)
     depth_xz, depth_zz = depth_pair(
         xz, lines_of(fields.at[1], lines), land, gram, inner_ref, outer_ref
     )
-    send_rows(packed, w, turned(xz))
-    copies[2].wait()
-    send_rows(packed, 0, turned(lines_of(fields.at[2], lines)))
-    copies[5].wait()
+    send_rows(packed, shared, 1, turned(xz))
     material = lines_of(material_ref, lines)
     down = turned(material)
-    counts = [
-        jnp.sum((down < layer).astype(jnp.float32), axis=0, keepdims=True) for layer in range(1, layers)
-    ]
-    rows = packed.shape[1] - 4 * w
+    counts = interfaces_of(down, layers)
+    own = 4 * share_rows(down.shape[0], groups)[0]
+    rows = packed.shape[1] - own
     counts = jnp.concatenate(counts + [counts[-1]] * (rows - layers + 1), axis=0)
     for d in range(groups):
-        packed[d, 4 * w :, :] = counts
-    step = [time_step * (1.0 / look_up(m, density_ref)) for m in material]
+        packed[d, own:, :] = counts
+    table = time_step * (1.0 / density_ref[...])
+    step = [look_up(m, table) for m in material]
+    copies[2].wait()
     copies[3].wait()
     copies[4].wait()
-    for first, i, d in ((2 * w, 3, depth_xz), (3 * w, 4, depth_zz)):
+    send_rows(packed, shared, 0, turned(lines_of(fields.at[2], lines)))
+    for slot, i, d in ((2, 3, depth_xz), (3, 4, depth_zz)):
         mixed = [v + s * x for v, s, x in zip(lines_of(fields.at[i], lines), step, d)]
-        send_rows(packed, first, turned(mixed))
-    scatter_blocks(place_ref, packed, out_refs)
-
-
-def scatter_blocks(place_ref, packed, out_refs):
+        send_rows(packed, shared, slot, turned(mixed))
+    place, half = place_ref[0], groups // 2
+    near, far, far_shared, land_out = out_refs[:half], out_refs[half:groups], out_refs[groups:-3], out_refs[-3]
+    land_out[...] = land.astype(jnp.float32)
+    out_refs[-2][...] = gram
+    lame, shear = lame_ref[...], shear_ref[...]
+    for i, row in enumerate((time_step * lame, time_step * (lame + 2.0 * shear), time_step * shear)):
+        out_refs[-1][i : i + 1, :] = jnp.pad(row, ((0, 0), (0, LANES - layers)))
+    for s, ref in enumerate(near):
+        ref[: packed.shape[1], :] = packed[place ^ s]
+        ref[packed.shape[1] :, :] = shared[(place ^ s) & (half - 1)]
+    for s, ref in enumerate(far):
+        ref[...] = packed[place ^ (s + half)]
+    for s, ref in enumerate(far_shared):
+        ref[...] = shared[(place ^ s) & (half - 1)]
+
+
+def step_of(interfaces, depth, step_ref):
+    step = jnp.full(depth.shape, step_ref[0], jnp.float32)
+    for layer in range(1, step_ref.shape[0]):
+        step = jnp.where(depth >= interfaces[layer - 1 : layer], step_ref[layer], step)
+    return jnp.concatenate([step, step], axis=0)
+
+
+def pencil_kernel(groups, place_ref, step_ref, even_ref, odd_ref, skew_ref, *rest):
+    in_refs, out_refs, (stress, slope, moving) = rest[:groups], rest[groups : 2 * groups], rest[2 * groups :]
+    n = in_refs[0].shape[1]
+    place = place_ref[0]
+    w = stress.shape[1] // 2
+    for s, ref in enumerate(in_refs):
+        stress[place ^ s] = ref[: 2 * w]
+    slopes = lateral(jnp.concatenate([stress[q] for q in range(groups)], axis=1), even_ref, odd_ref, skew_ref)
+    for q in range(groups):
+        slope[q] = slopes[:, q * n : (q + 1) * n]
+    depth = (lax.broadcasted_iota(jnp.int32, (w, n), 0) + place * w).astype(jnp.float32)
+    for s, ref in enumerate(in_refs):
+        step = step_of(ref[4 * w : 4 * w + step_ref.shape[0] - 1], depth, step_ref)
+        new = ref[2 * w : 4 * w] + step * slope[place ^ s]
+        out_refs[s][: 2 * w] = new
+        moving[place ^ s] = new
+    slopes = lateral(jnp.concatenate([moving[q] for q in range(groups)], axis=1), even_ref, odd_ref, skew_ref)
+    for q in range(groups):
+        slope[q] = slopes[:, q * n : (q + 1) * n]
     for s, ref in enumerate(out_refs):
-        ref[...] = packed[place_ref[0] ^ s]
-
-
-def collect_blocks(place_ref, in_refs, packed):
+        ref[2 * w :] = slope[place ^ s]
+
+
+def shared_kernel(groups, base, place_ref, step_ref, even_ref, odd_ref, skew_ref, *rest):
+    half = groups // 2
+    near, far, far_shared = rest[:half], rest[half:groups], rest[groups : groups + half]
+    done, out_refs, (stress, slope, moving) = rest[groups + half : 2 * groups], rest[2 * groups : -3], rest[-3:]
+    n = near[0].shape[1]
+    place = place_ref[0]
+    w = stress.shape[1] // 2
+    top = near[0].shape[0] - 4 * w
+    rows = step_ref.shape[0] - 1
+    held = top - -(-rows // 8) * 8
+    blocks = [(s, ref, ref, top) for s, ref in enumerate(near)] + [
+        (s + half, ref, raw, 0) for s, (ref, raw) in enumerate(zip(far, far_shared))
+    ]
+    for s, _, raw, start in blocks:
+        stress[place ^ s] = raw[start : start + 2 * w]
+    slopes = lateral(jnp.concatenate([stress[q] for q in range(groups)], axis=1), even_ref, odd_ref, skew_ref)
+    for q in range(groups):
+        slope[q] = slopes[:, q * n : (q + 1) * n]
+    depth = lax.broadcasted_iota(jnp.int32, (w, n), 0) + base + (place & (half - 1)) * w
+    depth = depth.astype(jnp.float32)
+    for s, ref, raw, start in blocks:
+        step = step_of(ref[held : held + rows], depth, step_ref)
+        new = raw[start + 2 * w : start + 4 * w] + step * slope[place ^ s]
+        if s < half:
+            out_refs[s][done[s].shape[0] : done[s].shape[0] + 2 * w] = new
+        moving[place ^ s] = new
+    slopes = lateral(jnp.concatenate([moving[q] for q in range(groups)], axis=1), even_ref, odd_ref, skew_ref)
+    for q in range(groups):
+        slope[q] = slopes[:, q * n : (q + 1) * n]
+    for s, ref in enumerate(out_refs):
+        ref[: done[s].shape[0]] = done[s][...]
+        ref[done[s].shape[0] + 2 * w :] = slope[place ^ s]
+
+
+def gather_rows(own_ref, shared_ref, slot):
+    own, shared = own_ref.shape[1] // 4, shared_ref.shape[1] // 4
+    field = jnp.concatenate(
+        [own_ref[d, slot * own : (slot + 1) * own, :] for d in range(own_ref.shape[0])]
+        + [shared_ref[r, slot * shared : (slot + 1) * shared, :] for r in range(shared_ref.shape[0])],
+        axis=0,
+    )
+    return [field[c * LANES : (c + 1) * LANES].T for c in range(field.shape[0] // LANES)]
+
+
+def last_kernel(
+    groups, place_ref, xx_ref, zz_ref, xz_ref, material_ref, inner_ref, outer_ref, land_ref, gram_ref, table_ref,
+    *rest,
+):
+    in_refs = rest[:groups]
+    new_vx, new_vz, new_xx_ref, new_zz_ref, new_xz_ref, settled, settled_shared = rest[groups:]
+    lines = land_ref.shape[0]
+    place, half, rows = place_ref[0], groups // 2, settled.shape[1]
     for s, ref in enumerate(in_refs):
-        packed[place_ref[0] ^ s] = ref[...]
-
-
-def pencil_kernel(groups, place_ref, step_ref, even_ref, odd_ref, skew_ref, *rest):
-    in_refs, out_refs, (arrived, leaving) = rest[:groups], rest[groups : 2 * groups], rest[2 * groups :]
-    n = in_refs[0].shape[1]
-    w = leaving.shape[1] // 4
-    collect_blocks(place_ref, in_refs, arrived)
-    x = jnp.concatenate([arrived[q, : 2 * w] for q in range(groups)], axis=1)
-    slopes = lateral(x, even_ref, odd_ref, skew_ref)
-    depth = (lax.broadcasted_iota(jnp.int32, (w, n), 0) + place_ref[0] * w).astype(jnp.float32)
-    moving = []
-    for q in range(groups):
-        step = jnp.full((w, n), step_ref[0], jnp.float32)
-        for layer in range(1, step_ref.shape[0]):
-            interface = arrived[q, 4 * w + layer - 1 : 4 * w + layer, :]
-            step = jnp.where(depth >= interface, step_ref[layer], step)
-        step = jnp.concatenate([step, step], axis=0)
-        new = arrived[q, 2 * w : 4 * w] + step * slopes[:, q * n : (q + 1) * n]
-        leaving[q, : 2 * w] = new
-        moving.append(new)
-    slopes = lateral(jnp.concatenate(moving, axis=1), even_ref, odd_ref, skew_ref)
-    for q in range(groups):
-        leaving[q, 2 * w :] = slopes[:, q * n : (q + 1) * n]
-    scatter_blocks(place_ref, leaving, out_refs)
-
-
-def gather_rows(ref, first, w):
-    field = jnp.concatenate([ref[d, first : first + w, :] for d in range(ref.shape[0])], axis=0)
-    return [field[c * LANES : (c + 1) * LANES].T for c in range(field.shape[0] // LANES)]
-
-
-def last_kernel(
-    groups, place_ref, lame_ref, shear_ref, xx_ref, zz_ref, xz_ref, material_ref, land_ref,
-    top_land_ref, top_sea_ref, bottom_ref, inner_ref, outer_ref, *rest,
-):
-    in_refs, (new_vx, new_vz, new_xx_ref, new_zz_ref, new_xz_ref, settled) = rest[:groups], rest[groups:]
-    lines = land_ref.shape[1]
-    w = settled.shape[1] // 4
-    collect_blocks(place_ref, in_refs, settled)
-    land = land_of(land_ref)
-    gram = gram_of(top_land_ref, top_sea_ref, bottom_ref, outer_ref.shape[1])
-    vx, vz, lateral_x, lateral_z = (gather_rows(settled, i * w, w) for i in range(4))
+        settled[place ^ s] = ref[:rows]
+    for s, ref in enumerate(in_refs[:half]):
+        settled_shared[(place ^ s) & (half - 1)] = ref[rows:]
+    land = land_ref[...] > 0
+    gram = gram_ref[...]
+    vx, vz, lateral_x, lateral_z = (gather_rows(settled, settled_shared, i) for i in range(4))
     put_lines(new_vx, vx)
     put_lines(new_vz, vz)
     dx, dz = depth_pair(vx, vz, land, gram, inner_ref, outer_ref)
     results = ([], [], [])
+    tables = [table_ref[i : i + 1, :] for i in range(3)]
     xx, zz, xz = lines_of(xx_ref, lines), lines_of(zz_ref, lines), lines_of(xz_ref, lines)
     material = lines_of(material_ref, lines)
     for c in range(len(vx)):
-        lame = look_up(material[c], lame_ref)
-        shear = look_up(material[c], shear_ref)
-        normal = lame + 2.0 * shear
-        new_xx = xx[c] + time_step * (normal * lateral_x[c] + lame * dz[c])
-        new_zz = zz[c] + time_step * (lame * lateral_x[c] + normal * dz[c])
-        new_xz = xz[c] + time_step * shear * (dx[c] + lateral_z[c])
+        lame, normal, shear = (look_up(material[c], table) for table in tables)
+        new_xx = xx[c] + (normal * lateral_x[c] + lame * dz[c])
+        new_zz = zz[c] + (lame * lateral_x[c] + normal * dz[c])
+        new_xz = xz[c] + shear * (dx[c] + lateral_z[c])
         if c == 0:
             surface = lax.broadcasted_iota(jnp.int32, new_zz.shape, 1) == 0
             new_zz = jnp.where(surface & land, 0.0, new_zz)
@@ -304,21 +384,15 @@
         out_specs=(VMEM,) * len(outs),
         scratch_shapes=list(scratch),
         cost_estimate=pl.CostEstimate(flops=flops, bytes_accessed=moved, transcendentals=0),
-        compiler_params=pltpu.CompilerParams(vmem_limit_bytes=40 << 20),
+        compiler_params=pltpu.CompilerParams(vmem_limit_bytes=16 << 20),
     )(*args)
 
 
-def hop_order(groups):
-    return list(range(groups // 2, groups)) + list(range(groups // 2 - 1, 0, -1))
-
-
-def exchange(blocks):
-    groups = len(blocks)
-    order = hop_order(groups)
+def hop(blocks, groups):
     moved = {}
-    for s in order:
-        moved[s] = lax.ppermute(blocks[s], "gx", [(i, i ^ s) for i in range(groups)])
-    return [blocks[0]] + [moved[s] for s in range(1, groups)]
+    for s, block in blocks.items():
+        moved[s] = lax.ppermute(block, "gx", [(i, i ^ s) for i in range(groups)])
+    return moved
 
 
 def body(
@@ -341,7 +415,8 @@
     width = lines * groups
     extra = continuation_land.shape[0]
     layers = density.shape[0]
-    w = depth // groups
+    own, shared = share_rows(depth, groups)
+    half = groups // 2
     f32 = jnp.float32
 
     def shape(*dims):
@@ -364,14 +439,19 @@
     place = lax.axis_index("gx").astype(jnp.int32).reshape(1)
     rows = -(-(layers - 1) // 8) * 8
     depth_flops = 2 * 2 * lines * depth * depth * 3
-    lateral_flops = 2 * 2 * w * width * width
+    lateral_flops = 2 * 2 * own * width * width
     stored = vx.shape
 
-    leaving = call(
+    near = range(half)
+    far = range(half, groups)
+    sent = call(
         first_kernel,
-        [shape(4 * w + rows, lines)] * groups,
-        [SMEM] + [HBM] * 13,
-        (place, *map(kept, (xz, zz, inner, xx, material, vx, vz, land, *grams, outer, density))),
+        [shape(4 * own + rows + 4 * shared, lines)] * half
+        + [shape(4 * own + rows, lines)] * half
+        + [shape(4 * shared, lines)] * half
+        + [shape(lines, LANES), shape(3 * outer.shape[1], LANES), shape(8, LANES)],
+        [SMEM] + [HBM] * 15,
+        (place, *map(kept, (xz, zz, inner, xx, material, vx, vz, land, *grams, outer, *(t.reshape(1, layers) for t in (density, lame_lambda, shear_modulus))))),
         depth_flops,
         [
             pltpu.VMEM((5, *stored), f32),
@@ -380,31 +460,58 @@
             pltpu.VMEM(land.shape, jnp.int32),
             *(pltpu.VMEM(g.shape, f32) for g in grams),
             pltpu.VMEM(outer.shape, outer.dtype),
-            pltpu.SMEM(density.shape, f32),
-            pltpu.VMEM((groups, 4 * w + rows, lines), f32),
-            pltpu.SemaphoreType.DMA((13,)),
+            *[pltpu.VMEM((1, layers), f32)] * 3,
+            pltpu.VMEM((groups, 4 * own + rows, lines), f32),
+            pltpu.VMEM((half, 4 * shared, lines), f32),
+            pltpu.SemaphoreType.DMA((15,)),
         ],
     )
-    arrived = exchange(leaving)
-    leaving = call(
+    got = hop({s: sent[s] for s in range(1, groups)}, groups)
+    raw = hop({s: sent[s + half] for s in far}, groups)
+    got[0] = sent[0]
+    ready = call(
         functools.partial(pencil_kernel, groups),
-        [shape(4 * w, lines)] * groups,
+        [shape(4 * own, lines)] * groups,
         [SMEM] * 2 + [VMEM] * (3 + groups),
-        (place, step, *fold_matrices, *arrived),
+        (place, step, *fold_matrices, *(got[s] for s in range(groups))),
         2 * lateral_flops,
-        [
-            pltpu.VMEM((groups, 4 * w + rows, lines), f32),
-            pltpu.VMEM((groups, 4 * w, lines), f32),
-        ],
-    )
-    arrived = exchange(leaving)
+        [pltpu.VMEM((groups, 2 * own, lines), f32)] * 3,
+    )
+    back = hop({s: ready[s] for s in far}, groups)
+    joined = call(
+        functools.partial(shared_kernel, groups, groups * own),
+        [shape(4 * own + 4 * shared, lines)] * half,
+        [SMEM] * 2 + [VMEM] * (3 + 2 * groups),
+        (
+            place,
+            step,
+            *fold_matrices,
+            *(got[s] for s in range(groups)),
+            *(raw[s] for s in far),
+            *(ready[s] for s in near),
+        ),
+        2 * lateral_flops,
+        [pltpu.VMEM((groups, 2 * shared, lines), f32)] * 3,
+    )
+    back |= hop({s: joined[s] for s in range(1, half)}, groups)
+    back[0] = joined[0]
     results = call(
         functools.partial(last_kernel, groups),
         [shape(*stored)] * 5,
-        [SMEM] * 3 + [VMEM] * (10 + groups),
-        (place, lame_lambda, shear_modulus, xx, zz, xz, material, land, *grams, inner, outer, *arrived),
+        [SMEM] + [VMEM] * (9 + groups),
+        (
+            place,
+            xx,
+            zz,
+            xz,
+            material,
+            inner,
+            outer,
+            *sent[-3:],
+            *(back[s] for s in range(groups)),
+        ),
         depth_flops,
-        [pltpu.VMEM((groups, 4 * w, lines), f32)],
+        [pltpu.VMEM((groups, 4 * own, lines), f32), pltpu.VMEM((half, 4 * shared, lines), f32)],
         False,
     )
     return tuple(x.reshape(velocity_x.shape) for x in results)
@@ -413,6 +520,8 @@
 def solution(mesh):
     field = P("gx", "gy", None)
     groups = mesh.shape["gx"]
+
+
     return jax.shard_map(
         functools.partial(body, groups),
         mesh=mesh,

time: 56.2 us -> 57.3 us (1.020); the launches traced: 55.2 us -> 57.2 us
  starting transfers between devices: 26.4 us -> 32.1 us
  waiting for transfers between devices: 20.2 us -> 16.1 us
    ppermute x14 -> x18, starting transfers between devices: 26.4 us -> 32.1 us  [hop(): moved[s] = lax.ppermute(block, 'gx', [(i, i ^ s) for i in range(groups)])]
    ppermute x14 -> x18, waiting for transfers between devices: 20.2 us -> 16.1 us  [hop(): moved[s] = lax.ppermute(block, 'gx', [(i, i ^ s) for i in range(groups)])]
    pallas_call x3 -> x4, Pallas kernels: 7.64 us -> 8.05 us  [call(): pl.pallas_call(kernel, out_shape=tuple((pltpu.VMEM(o.shape, o.dtype) if o...]
  transfers between devices with their start and end apart: 14 -> 18, of which waited for: 3 -> 4; matrix products, arithmetic and copies ran while one was open for 0% -> 0% of each run, Pallas kernels for 0% -> 6%
where the time goes in v2:
time: 57.3 us; the launch traced here: 57.2 us
  starting transfers between devices  32.1 us (56%)
  waiting for transfers between devices  16.1 us (28%)
  Pallas kernels  8.05 us (14%)
  between operations  0.81 us (1%)
    ppermute x18, starting transfers between devices, hop(): moved[s] = lax.ppermute(block, 'gx', [(i, i ^ s) for i in range(groups)])  32.1 us
    ppermute x18, waiting for transfers between devices, hop(): moved[s] = lax.ppermute(block, 'gx', [(i, i ^ s) for i in range(groups)])  16.1 us
    pallas_call x4, Pallas kernels, call(): pl.pallas_call(kernel, out_shape=tuple((pltpu.VMEM(o.shape, o.dtype) if o...  8.05 us
  transfers between devices with their start and end apart: 18, of which 4 were waited for; matrix products, arithmetic and copies ran while one was open for 0% of the time, Pallas kernels for 6%

profile of v2, /device:TPU:0, one launch (start us, length us, event | category | flops | bytes accessed | tf_op | source)
XLA Modules:
  0.0 57.2 jit_solution(1427300984665162221)
XLA Ops:
  0.6 0.0 copy-start
  0.7 0.0 copy-start.2
  0.7 0.0 copy-start.3
  0.7 2.7 %shard_map.209 = (f32[272,128]{1,0:T(8,128)S(1)}, f32[272,128]{1,0:T(8,128)S(1)}, f32[272,128]{1,0:T(8,128)S(1)}, f32[272,128]{1,0:T(8,128)S(1)}, f32[144,128]{1...) custom-call(s32[1]{0:T(128)} %bitcast.place_ref, ...), custom_call_target="tpu_custom_call" | custom-call | flops 226492416 | bytes 3060652 | tf_op jit(solution)/shard_map/pallas_call | solution.py:380
  3.4 4.1 %collective-permute-start.3 = (f32[144,128]{1,0:T(8,128)S(1)}, f32[144,128]{1,0:T(8,128)S(1)}, u32[]{:S(2)}, u32[]{:S(2)}) collective-permute-start(f32[144,128]{1,0:T(8,128)S(1)} %get-tuple-element.44), channel_id=1, source_target_pairs={{0,16},{4,20},{8,24},{12,28},{16,0},{20,4},{24,8},{28,12},{1,17},{... | collective-permute-start | bytes 221192 | tf_op jit(solution)/shard_map/ppermute | solution.py:394
  7.5 1.5 %collective-permute-start = (f32[272,128]{1,0:T(8,128)S(1)}, f32[272,128]{1,0:T(8,128)S(1)}, u32[]{:S(2)}, u32[]{:S(2)}) collective-permute-start(f32[272,128]{1,0:T(8,128)S(1)} %get-tuple-element.41), channel_id=1, source_target_pairs={{0,4},{4,0},{8,12},{12,8},{16,20},{20,16},{24,28},{28,24},{1,5},{5... | collective-permute-start | bytes 417800 | tf_op jit(solution)/shard_map/ppermute | solution.py:394
  9.0 1.6 %collective-permute-start.1 = (f32[272,128]{1,0:T(8,128)S(1)}, f32[272,128]{1,0:T(8,128)S(1)}, u32[]{:S(2)}, u32[]{:S(2)}) collective-permute-start(f32[272,128]{1,0:T(8,128)S(1)} %get-tuple-element.42), channel_id=1, source_target_pairs={{0,8},{4,12},{8,0},{12,4},{16,24},{20,28},{24,16},{28,20},{1,9},{5... | collective-permute-start | bytes 417800 | tf_op jit(solution)/shard_map/ppermute | solution.py:394
  10.6 0.3 collective-permute-start.4
  10.9 2.5 %collective-permute-start.5 = (f32[144,128]{1,0:T(8,128)S(1)}, f32[144,128]{1,0:T(8,128)S(1)}, u32[]{:S(2)}, u32[]{:S(2)}) collective-permute-start(f32[144,128]{1,0:T(8,128)S(1)} %get-tuple-element.46), channel_id=1, source_target_pairs={{0,24},{4,28},{8,16},{12,20},{16,8},{20,12},{24,0},{28,4},{1,25},{... | collective-permute-start | bytes 221192 | tf_op jit(solution)/shard_map/ppermute | solution.py:394
  13.4 2.8 %collective-permute-start.6 = (f32[144,128]{1,0:T(8,128)S(1)}, f32[144,128]{1,0:T(8,128)S(1)}, u32[]{:S(2)}, u32[]{:S(2)}) collective-permute-start(f32[144,128]{1,0:T(8,128)S(1)} %get-tuple-element.47), channel_id=1, source_target_pairs={{0,28},{4,24},{8,20},{12,16},{16,12},{20,8},{24,4},{28,0},{1,29},{... | collective-permute-start | bytes 221192 | tf_op jit(solution)/shard_map/ppermute | solution.py:394
  16.2 5.7 %collective-permute-done.4.rest_5_ = f32[144,128]{1,0:T(8,128)S(1)} collective-permute-done((f32[144,128]{1,0:T(8,128)S(1)}, f32[144,128]{1,0:T(8,128)S(1)}, u32[]{:S(2)}, u32[]{:S(2)}) %collective-permute-start.4) | collective-permute-done | bytes 73760 | tf_op jit(solution)/shard_map/ppermute | solution.py:394
  21.9 3.0 %collective-permute-start.8 = (f32[128,128]{1,0:T(8,128)S(1)}, f32[128,128]{1,0:T(8,128)S(1)}, u32[]{:S(2)}, u32[]{:S(2)}) collective-permute-start(f32[128,128]{1,0:T(8,128)S(1)} %get-tuple-element.49), channel_id=1, source_target_pairs={{0,20},{4,16},{8,28},{12,24},{16,4},{20,0},{24,12},{28,8},{1,21},{... | collective-permute-start | bytes 196616 | tf_op jit(solution)/shard_map/ppermute | solution.py:394
  24.9 2.2 %collective-permute-start.9 = (f32[128,128]{1,0:T(8,128)S(1)}, f32[128,128]{1,0:T(8,128)S(1)}, u32[]{:S(2)}, u32[]{:S(2)}) collective-permute-start(f32[128,128]{1,0:T(8,128)S(1)} %get-tuple-element.50), channel_id=1, source_target_pairs={{0,24},{4,28},{8,16},{12,20},{16,8},{20,12},{24,0},{28,4},{1,25},{... | collective-permute-start | bytes 196616 | tf_op jit(solution)/shard_map/ppermute | solution.py:394
  27.1 2.4 %collective-permute-start.10 = (f32[128,128]{1,0:T(8,128)S(1)}, f32[128,128]{1,0:T(8,128)S(1)}, u32[]{:S(2)}, u32[]{:S(2)}) collective-permute-start(f32[128,128]{1,0:T(8,128)S(1)} %get-tuple-element.51), channel_id=1, source_target_pairs={{0,28},{4,24},{8,20},{12,16},{16,12},{20,8},{24,4},{28,0},{1,29},{... | collective-permute-start | bytes 196616 | tf_op jit(solution)/shard_map/ppermute | solution.py:394
  29.6 0.4 collective-permute-start.2
  30.0 5.7 %collective-permute-done.2.rest_3_ = f32[272,128]{1,0:T(8,128)S(1)} collective-permute-done((f32[272,128]{1,0:T(8,128)S(1)}, f32[272,128]{1,0:T(8,128)S(1)}, u32[]{:S(2)}, u32[]{:S(2)}) %collective-permute-start.2) | collective-permute-done | bytes 139296 | tf_op jit(solution)/shard_map/ppermute | solution.py:394
  35.7 1.8 %shard_map.210 = (f32[128,128]{1,0:T(8,128)S(1)}, f32[128,128]{1,0:T(8,128)S(1)}, f32[128,128]{1,0:T(8,128)S(1)}, f32[128,128]{1,0:T(8,128)S(1)}, f32[128,128]{1...) custom-call(s32[1]{0:T(128)} %bitcast.place_ref, ...), custom_call_target="tpu_custom_call" | custom-call | flops 268435456 | bytes 2949188 | tf_op jit(solution)/shard_map/pallas_call | solution.py:380
  37.4 1.3 %collective-permute-start.14 = (f32[128,128]{1,0:T(8,128)S(1)}, f32[128,128]{1,0:T(8,128)S(1)}, u32[]{:S(2)}, u32[]{:S(2)}) collective-permute-start(f32[128,128]{1,0:T(8,128)S(1)} %get-tuple-element.60), channel_id=1, source_target_pairs={{0,16},{4,20},{8,24},{12,28},{16,0},{20,4},{24,8},{28,12},{1,17},{... | collective-permute-start | bytes 196616 | tf_op jit(solution)/shard_map/ppermute | solution.py:394
  38.8 1.8 %collective-permute-start.15 = (f32[128,128]{1,0:T(8,128)S(1)}, f32[128,128]{1,0:T(8,128)S(1)}, u32[]{:S(2)}, u32[]{:S(2)}) collective-permute-start(f32[128,128]{1,0:T(8,128)S(1)} %get-tuple-element.61), channel_id=1, source_target_pairs={{0,20},{4,16},{8,28},{12,24},{16,4},{20,0},{24,12},{28,8},{1,21},{... | collective-permute-start | bytes 196616 | tf_op jit(solution)/shard_map/ppermute | solution.py:394
  40.6 0.0 copy-start.1
  40.6 0.0 copy-start.4
  40.6 0.0 copy-start.5
  40.7 0.0 copy-start.8
  40.7 1.7 %shard_map.211 = (f32[256,128]{1,0:T(8,128)S(1)}, f32[256,128]{1,0:T(8,128)S(1)}, f32[256,128]{1,0:T(8,128)S(1)}, f32[256,128]{1,0:T(8,128)S(1)}) custom-call(s32[1]{0:T(128)} %bitcast.place_ref, f32[16]{0:T(128)S(1)} %divide_multiply_fusion.step_ref, bf16[2,256,256]{2,1,0:T(8,128)(2,1)S(1)} %copy-done.3, bf16[2,256,256]{2,1,0:T(8,128)(2,1)S(1)} %copy-done.2, ...), custom_call_target="tpu_custom_call" | custom-call | flops 268435456 | bytes 3473476 | tf_op jit(solution)/shard_map/pallas_call | solution.py:380
  42.4 1.4 %collective-permute-start.11 = (f32[256,128]{1,0:T(8,128)S(1)}, f32[256,128]{1,0:T(8,128)S(1)}, u32[]{:S(2)}, u32[]{:S(2)}) collective-permute-start(f32[256,128]{1,0:T(8,128)S(1)} %get-tuple-element.57), channel_id=1, source_target_pairs={{0,4},{4,0},{8,12},{12,8},{16,20},{20,16},{24,28},{28,24},{1,5},{5... | collective-permute-start | bytes 393224 | tf_op jit(solution)/shard_map/ppermute | solution.py:394
  43.8 0.3 collective-permute-start.12
  44.1 1.8 %collective-permute-start.13 = (f32[256,128]{1,0:T(8,128)S(1)}, f32[256,128]{1,0:T(8,128)S(1)}, u32[]{:S(2)}, u32[]{:S(2)}) collective-permute-start(f32[256,128]{1,0:T(8,128)S(1)} %get-tuple-element.59), channel_id=1, source_target_pairs={{0,12},{4,8},{8,4},{12,0},{16,28},{20,24},{24,20},{28,16},{1,13},{... | collective-permute-start | bytes 393224 | tf_op jit(solution)/shard_map/ppermute | solution.py:394
  46.0 2.3 %collective-permute-start.16 = (f32[128,128]{1,0:T(8,128)S(1)}, f32[128,128]{1,0:T(8,128)S(1)}, u32[]{:S(2)}, u32[]{:S(2)}) collective-permute-start(f32[128,128]{1,0:T(8,128)S(1)} %get-tuple-element.62), channel_id=1, source_target_pairs={{0,24},{4,28},{8,16},{12,20},{16,8},{20,12},{24,0},{28,4},{1,25},{... | collective-permute-start | bytes 196616 | tf_op jit(solution)/shard_map/ppermute | solution.py:394
  48.3 2.3 %collective-permute-start.17 = (f32[128,128]{1,0:T(8,128)S(1)}, f32[128,128]{1,0:T(8,128)S(1)}, u32[]{:S(2)}, u32[]{:S(2)}) collective-permute-start(f32[128,128]{1,0:T(8,128)S(1)} %get-tuple-element.63), channel_id=1, source_target_pairs={{0,28},{4,24},{8,20},{12,16},{16,12},{20,8},{24,4},{28,0},{1,29},{... | collective-permute-start | bytes 196616 | tf_op jit(solution)/shard_map/ppermute | solution.py:394
  50.6 2.3 %collective-permute-done.16.rest_6_ = f32[128,128]{1,0:T(8,128)S(1)} collective-permute-done((f32[128,128]{1,0:T(8,128)S(1)}, f32[128,128]{1,0:T(8,128)S(1)}, u32[]{:S(2)}, u32[]{:S(2)}) %collective-permute-start.16) | collective-permute-done | bytes 65568 | tf_op jit(solution)/shard_map/ppermute | solution.py:394
  52.8 2.4 %collective-permute-done.17.rest_7_ = f32[128,128]{1,0:T(8,128)S(1)} collective-permute-done((f32[128,128]{1,0:T(8,128)S(1)}, f32[128,128]{1,0:T(8,128)S(1)}, u32[]{:S(2)}, u32[]{:S(2)}) %collective-permute-start.17) | collective-permute-done | bytes 65568 | tf_op jit(solution)/shard_map/ppermute | solution.py:394
  55.3 1.8 %shard_map.212 = (f32[384,128]{1,0:T(8,128)}, f32[384,128]{1,0:T(8,128)}, f32[384,128]{1,0:T(8,128)}, f32[384,128]{1,0:T(8,128)}, f32[384,128]{1,0:T(8,128)}) custom-call(s32[1]{0:T(128)} %bitcast.place_ref, f32[384,128]{1,0:T(8,128)S(1)} %bitcast.17, f32[384,128]{1,0:T(8,128)S(1)} %bitcast.19, f32[384,128]{1,0:T(8,128)S(1)} %bitcast.21, ...), custom_call_target="tpu_custom_call" | custom-call | flops 226492416 | bytes 3313668 | tf_op jit(solution)/shard_map/pallas_call | solution.py:380
  (29 shorter events, 0.1 us)
Async XLA Ops:
  0.6 35.0 %copy-start = (bf16[2,512,512]{2,1,0:T(8,128)(2,1)S(1)}, bf16[2,512,512]{2,1,0:T(8,128)(2,1)}, u32[]{:S(2)}) copy-start(bf16[2,512,512]{2,1,0:T(8,128)(2,1)} %constant.24.clone.skew_ref) | copy-start | bytes 3145732
  0.7 35.0 %copy-start.2 = (bf16[2,256,256]{2,1,0:T(8,128)(2,1)S(1)}, bf16[2,256,256]{2,1,0:T(8,128)(2,1)}, u32[]{:S(2)}) copy-start(bf16[2,256,256]{2,1,0:T(8,128)(2,1)} %constant.23.clone.odd_ref) | copy-start | bytes 786436
  0.7 35.0 %copy-start.3 = (bf16[2,256,256]{2,1,0:T(8,128)(2,1)S(1)}, bf16[2,256,256]{2,1,0:T(8,128)(2,1)}, u32[]{:S(2)}) copy-start(bf16[2,256,256]{2,1,0:T(8,128)(2,1)} %constant.22.clone.even_ref) | copy-start | bytes 786436
  3.4 10.0 %collective-permute-start.3 = (f32[144,128]{1,0:T(8,128)S(1)}, f32[144,128]{1,0:T(8,128)S(1)}, u32[]{:S(2)}, u32[]{:S(2)}) collective-permute-start(f32[144,128]{1,0:T(8,128)S(1)} %get-tuple-element.44), channel_id=1, source_target_pairs={{0,16},{4,20},{8,24},{12,28},{16,0},{20,4},{24,8},{28,12},{1,17},{... | collective-permute-start | bytes 221192 | tf_op jit(solution)/shard_map/ppermute | solution.py:394
  7.5 19.6 %collective-permute-start = (f32[272,128]{1,0:T(8,128)S(1)}, f32[272,128]{1,0:T(8,128)S(1)}, u32[]{:S(2)}, u32[]{:S(2)}) collective-permute-start(f32[272,128]{1,0:T(8,128)S(1)} %get-tuple-element.41), channel_id=1, source_target_pairs={{0,4},{4,0},{8,12},{12,8},{16,20},{20,16},{24,28},{28,24},{1,5},{5... | collective-permute-start | bytes 417800 | tf_op jit(solution)/shard_map/ppermute | solution.py:394
  9.0 20.5 %collective-permute-start.1 = (f32[272,128]{1,0:T(8,128)S(1)}, f32[272,128]{1,0:T(8,128)S(1)}, u32[]{:S(2)}, u32[]{:S(2)}) collective-permute-start(f32[272,128]{1,0:T(8,128)S(1)} %get-tuple-element.42), channel_id=1, source_target_pairs={{0,8},{4,12},{8,0},{12,4},{16,24},{20,28},{24,16},{28,20},{1,9},{5... | collective-permute-start | bytes 417800 | tf_op jit(solution)/shard_map/ppermute | solution.py:394
  10.6 11.3 %collective-permute-start.4 = (f32[144,128]{1,0:T(8,128)S(1)}, f32[144,128]{1,0:T(8,128)S(1)}, u32[]{:S(2)}, u32[]{:S(2)}) collective-permute-start(f32[144,128]{1,0:T(8,128)S(1)} %get-tuple-element.45), channel_id=1, source_target_pairs={{0,20},{4,16},{8,28},{12,24},{16,4},{20,0},{24,12},{28,8},{1,21},{... | collective-permute-start | bytes 221192 | tf_op jit(solution)/shard_map/ppermute | solution.py:394
  10.9 11.0 %collective-permute-start.5 = (f32[144,128]{1,0:T(8,128)S(1)}, f32[144,128]{1,0:T(8,128)S(1)}, u32[]{:S(2)}, u32[]{:S(2)}) collective-permute-start(f32[144,128]{1,0:T(8,128)S(1)} %get-tuple-element.46), channel_id=1, source_target_pairs={{0,24},{4,28},{8,16},{12,20},{16,8},{20,12},{24,0},{28,4},{1,25},{... | collective-permute-start | bytes 221192 | tf_op jit(solution)/shard_map/ppermute | solution.py:394
  13.4 11.5 %collective-permute-start.6 = (f32[144,128]{1,0:T(8,128)S(1)}, f32[144,128]{1,0:T(8,128)S(1)}, u32[]{:S(2)}, u32[]{:S(2)}) collective-permute-start(f32[144,128]{1,0:T(8,128)S(1)} %get-tuple-element.47), channel_id=1, source_target_pairs={{0,28},{4,24},{8,20},{12,16},{16,12},{20,8},{24,4},{28,0},{1,29},{... | collective-permute-start | bytes 221192 | tf_op jit(solution)/shard_map/ppermute | solution.py:394
  21.9 16.9 %collective-permute-start.7 = (f32[128,128]{1,0:T(8,128)S(1)}, f32[128,128]{1,0:T(8,128)S(1)}, u32[]{:S(2)}, u32[]{:S(2)}) collective-permute-start(f32[128,128]{1,0:T(8,128)S(1)} %get-tuple-element.48), channel_id=1, source_target_pairs={{0,16},{4,20},{8,24},{12,28},{16,0},{20,4},{24,8},{28,12},{1,17},{... | collective-permute-start | bytes 196616 | tf_op jit(solution)/shard_map/ppermute | solution.py:394
  21.9 18.7 %collective-permute-start.8 = (f32[128,128]{1,0:T(8,128)S(1)}, f32[128,128]{1,0:T(8,128)S(1)}, u32[]{:S(2)}, u32[]{:S(2)}) collective-permute-start(f32[128,128]{1,0:T(8,128)S(1)} %get-tuple-element.49), channel_id=1, source_target_pairs={{0,20},{4,16},{8,28},{12,24},{16,4},{20,0},{24,12},{28,8},{1,21},{... | collective-permute-start | bytes 196616 | tf_op jit(solution)/shard_map/ppermute | solution.py:394
  24.9 15.7 %collective-permute-start.9 = (f32[128,128]{1,0:T(8,128)S(1)}, f32[128,128]{1,0:T(8,128)S(1)}, u32[]{:S(2)}, u32[]{:S(2)}) collective-permute-start(f32[128,128]{1,0:T(8,128)S(1)} %get-tuple-element.50), channel_id=1, source_target_pairs={{0,24},{4,28},{8,16},{12,20},{16,8},{20,12},{24,0},{28,4},{1,25},{... | collective-permute-start | bytes 196616 | tf_op jit(solution)/shard_map/ppermute | solution.py:394
  27.1 2.9 %copy-start.9 = (f32[16]{0:T(128)S(1)}, f32[16]{0:T(128)}, u32[]{:S(2)}) copy-start(f32[16]{0:T(128)} %param.25) | copy-start | bytes 196
  27.1 13.5 %collective-permute-start.10 = (f32[128,128]{1,0:T(8,128)S(1)}, f32[128,128]{1,0:T(8,128)S(1)}, u32[]{:S(2)}, u32[]{:S(2)}) collective-permute-start(f32[128,128]{1,0:T(8,128)S(1)} %get-tuple-element.51), channel_id=1, source_target_pairs={{0,28},{4,24},{8,20},{12,16},{16,12},{20,8},{24,4},{28,0},{1,29},{... | collective-permute-start | bytes 196616 | tf_op jit(solution)/shard_map/ppermute | solution.py:394
  29.6 6.1 %collective-permute-start.2 = (f32[272,128]{1,0:T(8,128)S(1)}, f32[272,128]{1,0:T(8,128)S(1)}, u32[]{:S(2)}, u32[]{:S(2)}) collective-permute-start(f32[272,128]{1,0:T(8,128)S(1)} %get-tuple-element.43), channel_id=1, source_target_pairs={{0,12},{4,8},{8,4},{12,0},{16,28},{20,24},{24,20},{28,16},{1,13},{... | collective-permute-start | bytes 417800 | tf_op jit(solution)/shard_map/ppermute | solution.py:394
  37.4 8.5 %collective-permute-start.14 = (f32[128,128]{1,0:T(8,128)S(1)}, f32[128,128]{1,0:T(8,128)S(1)}, u32[]{:S(2)}, u32[]{:S(2)}) collective-permute-start(f32[128,128]{1,0:T(8,128)S(1)} %get-tuple-element.60), channel_id=1, source_target_pairs={{0,16},{4,20},{8,24},{12,28},{16,0},{20,4},{24,8},{28,12},{1,17},{... | collective-permute-start | bytes 196616 | tf_op jit(solution)/shard_map/ppermute | solution.py:394
  38.8 9.5 %collective-permute-start.15 = (f32[128,128]{1,0:T(8,128)S(1)}, f32[128,128]{1,0:T(8,128)S(1)}, u32[]{:S(2)}, u32[]{:S(2)}) collective-permute-start(f32[128,128]{1,0:T(8,128)S(1)} %get-tuple-element.61), channel_id=1, source_target_pairs={{0,20},{4,16},{8,28},{12,24},{16,4},{20,0},{24,12},{28,8},{1,21},{... | collective-permute-start | bytes 196616 | tf_op jit(solution)/shard_map/ppermute | solution.py:394
  40.6 14.7 %copy-start.1 = (bf16[2,384,384]{2,1,0:T(8,128)(2,1)S(1)}, bf16[2,384,384]{2,1,0:T(8,128)(2,1)}, u32[]{:S(2)}) copy-start(bf16[2,384,384]{2,1,0:T(8,128)(2,1)} %constant.20.clone.inner_hbm.inner_ref) | copy-start | bytes 1769476
  40.6 14.7 %copy-start.4 = (f32[128,1,384]{2,1,0:T(1,128)S(1)}, f32[128,1,384]{2,1,0:T(1,128)}, u32[]{:S(2)}) copy-start(f32[128,1,384]{2,1,0:T(1,128)} %param.20) | copy-start | bytes 589828
  40.6 14.7 %copy-start.5 = (f32[128,1,384]{2,1,0:T(1,128)S(1)}, f32[128,1,384]{2,1,0:T(1,128)}, u32[]{:S(2)}) copy-start(f32[128,1,384]{2,1,0:T(1,128)} %param.21) | copy-start | bytes 589828
  40.6 14.7 %copy-start.6 = (f32[128,1,384]{2,1,0:T(1,128)S(1)}, f32[128,1,384]{2,1,0:T(1,128)}, u32[]{:S(2)}) copy-start(f32[128,1,384]{2,1,0:T(1,128)} %param.22) | copy-start | bytes 589828
  40.7 14.7 %copy-start.7 = (s32[128,1,384]{2,1,0:T(1,128)S(1)}, s32[128,1,384]{2,1,0:T(1,128)}, u32[]{:S(2)}) copy-start(s32[128,1,384]{2,1,0:T(1,128)} %param.23) | copy-start | bytes 589828
  40.7 14.7 %copy-start.8 = (bf16[2,32,384]{2,1,0:T(8,128)(2,1)S(1)}, bf16[2,32,384]{2,1,0:T(8,128)(2,1)}, u32[]{:S(2)}) copy-start(bf16[2,32,384]{2,1,0:T(8,128)(2,1)} %constant.21.clone.outer_hbm.outer_ref) | copy-start | bytes 147460
  42.4 12.8 %collective-permute-start.11 = (f32[256,128]{1,0:T(8,128)S(1)}, f32[256,128]{1,0:T(8,128)S(1)}, u32[]{:S(2)}, u32[]{:S(2)}) collective-permute-start(f32[256,128]{1,0:T(8,128)S(1)} %get-tuple-element.57), channel_id=1, source_target_pairs={{0,4},{4,0},{8,12},{12,8},{16,20},{20,16},{24,28},{28,24},{1,5},{5... | collective-permute-start | bytes 393224 | tf_op jit(solution)/shard_map/ppermute | solution.py:394
  43.8 11.5 %collective-permute-start.12 = (f32[256,128]{1,0:T(8,128)S(1)}, f32[256,128]{1,0:T(8,128)S(1)}, u32[]{:S(2)}, u32[]{:S(2)}) collective-permute-start(f32[256,128]{1,0:T(8,128)S(1)} %get-tuple-element.58), channel_id=1, source_target_pairs={{0,8},{4,12},{8,0},{12,4},{16,24},{20,28},{24,16},{28,20},{1,9},{5... | collective-permute-start | bytes 393224 | tf_op jit(solution)/shard_map/ppermute | solution.py:394
  44.1 11.1 %collective-permute-start.13 = (f32[256,128]{1,0:T(8,128)S(1)}, f32[256,128]{1,0:T(8,128)S(1)}, u32[]{:S(2)}, u32[]{:S(2)}) collective-permute-start(f32[256,128]{1,0:T(8,128)S(1)} %get-tuple-element.59), channel_id=1, source_target_pairs={{0,12},{4,8},{8,4},{12,0},{16,28},{20,24},{24,20},{28,16},{1,13},{... | collective-permute-start | bytes 393224 | tf_op jit(solution)/shard_map/ppermute | solution.py:394
  46.0 6.8 %collective-permute-start.16 = (f32[128,128]{1,0:T(8,128)S(1)}, f32[128,128]{1,0:T(8,128)S(1)}, u32[]{:S(2)}, u32[]{:S(2)}) collective-permute-start(f32[128,128]{1,0:T(8,128)S(1)} %get-tuple-element.62), channel_id=1, source_target_pairs={{0,24},{4,28},{8,16},{12,20},{16,8},{20,12},{24,0},{28,4},{1,25},{... | collective-permute-start | bytes 196616 | tf_op jit(solution)/shard_map/ppermute | solution.py:394
  48.3 7.0 %collective-permute-start.17 = (f32[128,128]{1,0:T(8,128)S(1)}, f32[128,128]{1,0:T(8,128)S(1)}, u32[]{:S(2)}, u32[]{:S(2)}) collective-permute-start(f32[128,128]{1,0:T(8,128)S(1)} %get-tuple-element.63), channel_id=1, source_target_pairs={{0,28},{4,24},{8,20},{12,16},{16,12},{20,8},{24,4},{28,0},{1,29},{... | collective-permute-start | bytes 196616 | tf_op jit(solution)/shard_map/ppermute | solution.py:394
